TPU v7x, 32 devices: a whole 2x2x4 slice. The times are simulated.
32 devices in a mesh: dp: 2 (over core), row: 4 (over y, x), col: 4 (over z).
Axes of the slice: x: 2, y: 2, z: 4, core: 2. Of those that a mesh axis runs over, the one named last changes fastest.
Arguments:
- tokens: bfloat16 [768, 8192], P('row', ('dp', 'col')), may hold values from -6 to 6
- prefix: int32 [8], P(('dp', 'row')), may hold values from 102 to 512, as said below
- ln1_gain: float32 [768], replicated, may hold values from 0.5 to 1.5
- ln1_bias: float32 [768], replicated, may hold values from -3 to 3
- w_qkv: bfloat16 [3, 768, 768], P(None, 'row', 'col'), may hold values from -0.21875 to 0.21875
- qv_bias: float32 [2, 768], replicated, may hold values from -3 to 3
- w_out: bfloat16 [768, 768], P('col', 'row'), may hold values from -0.875 to 0.875
- out_bias: float32 [768], replicated, may hold values from -3 to 3
- ln2_gain: float32 [768], replicated, may hold values from 0.5 to 1.5
- ln2_bias: float32 [768], replicated, may hold values from -3 to 3
- w_fc: bfloat16 [768, 3072], P('row', 'col'), may hold values from -0.21875 to 0.21875
- fc_bias: float32 [3072], replicated, may hold values from -3 to 3
- w_proj: bfloat16 [768, 3072], P('row', 'col'), may hold values from -0.109375 to 0.109375
- proj_bias: float32 [768], replicated, may hold values from -3 to 3
- cotangent: bfloat16 [768, 8192], P('row', ('dp', 'col')), may hold values from -6 to 6
Outputs:
- output: bfloat16 [768, 8192], P('row', ('dp', 'col'))
- input_grad: float32 [768, 8192], P('row', ('dp', 'col'))
- ln1_gain_grad: float32 [768], replicated
- ln1_bias_grad: float32 [768], replicated
- w_qkv_grad: float32 [3, 768, 768], P(None, 'row', 'col')
- qv_bias_grad: float32 [2, 768], replicated
- w_out_grad: float32 [768, 768], P('col', 'row')
- out_bias_grad: float32 [768], replicated
- ln2_gain_grad: float32 [768], replicated
- ln2_bias_grad: float32 [768], replicated
- w_fc_grad: float32 [768, 3072], P('row', 'col')
- fc_bias_grad: float32 [3072], replicated
- w_proj_grad: float32 [768, 3072], P('row', 'col')
- proj_bias_grad: float32 [768], replicated
Inputs may be any that keep to these rules, and one draw needn't show every extreme that they name: `prefix`: in every draw some sequence has exactly 102 and some other exactly 512.
All inputs are finite; a program needn't handle non-finite values.
Results may differ from a plain program's by a relative error of at most 0.012.
Values may be sent and summed in bfloat16 or wider, within the bound.
A program may use at most 256 MiB of HBM per device.

v0:
```python
import jax
import jax.numpy as jnp
from jax import lax
from jax.sharding import PartitionSpec as P

D = 768
FF = 3072
HEAD_DIM = 64
LEN = 1024


epsilon = 1e-05
masked_score = -1e30


def feature_totals(values):
    return lax.psum(values, "row")


def column_rows(values):
    return lax.all_gather(values, "col", axis=0, tiled=True)


def row_rows(values):
    return lax.all_gather(values, "row", axis=0, tiled=True)


def summed_over_row(term_fn, row_count):
    return lax.psum_scatter(
        term_fn(jnp.int32(0), row_count * lax.axis_size("row")),
        "row",
        scatter_dimension=0,
        tiled=True,
    )


def summed_over_col(term_fn, row_count):
    return lax.psum_scatter(
        term_fn(jnp.int32(0), row_count * lax.axis_size("col")),
        "col",
        scatter_dimension=0,
        tiled=True,
    )


def take_portion(complete, position, portion_size, along):
    return lax.dynamic_slice_in_dim(complete, position * portion_size, portion_size, along)


def place_portion(portion, position, full_size, along):
    zeroed_shape = portion.shape[:along] + (full_size,) + portion.shape[along + 1 :]
    zeroed = jnp.zeros(zeroed_shape, jnp.float32)
    return lax.dynamic_update_slice_in_dim(zeroed, portion, position * portion.shape[along], along)


def gelu_tanh(values):
    return jax.nn.gelu(values, approximate=True)


def norm_forward(values, norm_gain, norm_offset, totals_fn):
    plain_sum, square_sum = totals_fn((jnp.sum(values, axis=1), jnp.sum(values * values, axis=1)))
    center = (plain_sum / D)[:, None]
    inverse = lax.rsqrt(square_sum[:, None] / D - center * center + epsilon)
    unit_rows = (values - center) * inverse
    return (unit_rows * norm_gain + norm_offset, unit_rows, inverse)


def norm_backward(grad_rows, unit_rows, inverse, norm_gain, totals_fn):
    scaled = grad_rows * norm_gain
    plain_sum, cross_sum = totals_fn((jnp.sum(scaled, axis=1), jnp.sum(scaled * unit_rows, axis=1)))
    return inverse * (scaled - (plain_sum / D)[:, None] - unit_rows * (cross_sum / D)[:, None])


def split_heads(flat_rows):
    return flat_rows.reshape(LEN, flat_rows.shape[1] // HEAD_DIM, HEAD_DIM)


def scores_of(queries, keys_block, limit_value):
    raw_scores = jnp.einsum("qhe,khe->hqk", queries, keys_block, preferred_element_type=jnp.float32)
    raw_scores = raw_scores * HEAD_DIM ** (-0.5)
    places = jnp.arange(LEN, dtype=jnp.int32)
    visible = (places[None, :] <= places[:, None]) | (places[None, :] < limit_value)
    return jnp.where(visible[None], raw_scores, masked_score)


def attend_forward(packed):
    block_rows, limit_value = packed
    queries = split_heads(block_rows[:, 0])
    keys_block = split_heads(block_rows[:, 1])
    values_block = split_heads(block_rows[:, 2])
    scores = scores_of(queries, keys_block, limit_value)
    largest = jnp.max(scores, axis=-1, keepdims=True)
    weights = jnp.exp(scores - largest)
    row_totals = jnp.sum(weights, axis=-1, keepdims=True)
    probs = (weights / row_totals).astype(jnp.bfloat16)
    mixed = jnp.einsum("hqk,khe->qhe", probs, values_block, preferred_element_type=jnp.float32)
    return (mixed.reshape(LEN, -1).astype(jnp.bfloat16), (largest + jnp.log(row_totals))[..., 0])


def attend_backward(packed):
    block_rows, limit_value, log_total, out_grad = packed
    queries = split_heads(block_rows[:, 0])
    keys_block = split_heads(block_rows[:, 1])
    values_block = split_heads(block_rows[:, 2])
    scores = scores_of(queries, keys_block, limit_value)
    probs = jnp.exp(scores - log_total[..., None])
    probs_low = probs.astype(jnp.bfloat16)
    grad_heads = split_heads(out_grad)
    weight_grad = jnp.einsum(
        "qhe,khe->hqk", grad_heads, values_block, preferred_element_type=jnp.float32
    )
    row_inner = jnp.sum(probs * weight_grad, axis=-1, keepdims=True)
    score_grad = (probs * (weight_grad - row_inner)).astype(jnp.bfloat16)
    query_grad = jnp.einsum(
        "hqk,khe->qhe", score_grad, keys_block, preferred_element_type=jnp.float32
    )
    key_grad = jnp.einsum("hqk,qhe->khe", score_grad, queries, preferred_element_type=jnp.float32)
    value_grad = jnp.einsum(
        "hqk,qhe->khe", probs_low, grad_heads, preferred_element_type=jnp.float32
    )
    score_factor = HEAD_DIM ** (-0.5)
    stacked = jnp.stack(
        [
            (query_grad * score_factor).reshape(LEN, -1),
            (key_grad * score_factor).reshape(LEN, -1),
            value_grad.reshape(LEN, -1),
        ],
        axis=1,
    )
    return stacked.astype(jnp.bfloat16)


def on_device(
    tokens,
    prefix,
    ln1_gain,
    ln1_bias,
    w_qkv,
    qv_bias,
    w_out,
    out_bias,
    ln2_gain,
    ln2_bias,
    w_fc,
    fc_bias,
    w_proj,
    proj_bias,
    cotangent,
):
    row_place = lax.axis_index("row")
    col_place = lax.axis_index("col")
    row_devices = lax.axis_size("row")
    col_devices = lax.axis_size("col")
    width_row, local_rows = tokens.shape
    width_col = w_qkv.shape[2]
    hidden_col = w_fc.shape[1]
    seq_rows = local_rows * col_devices // row_devices
    seq_count = seq_rows // LEN
    residual = tokens.T.astype(jnp.float32)
    cotangent_local = cotangent.T
    first_gain = take_portion(ln1_gain, row_place, width_row, 0)
    first_normed, first_unit, first_inverse = norm_forward(
        residual, first_gain, take_portion(ln1_bias, row_place, width_row, 0), feature_totals
    )
    first_gathered = column_rows(first_normed.astype(jnp.bfloat16))

    def qkv_term(first_row, row_count):
        return jnp.einsum("td,sde->tse", first_gathered, w_qkv, preferred_element_type=jnp.float32)

    bias_col = take_portion(qv_bias, col_place, width_col, 1)
    bias_rows = jnp.stack([bias_col[0], jnp.zeros_like(bias_col[0]), bias_col[1]])
    qkv_sum = summed_over_row(qkv_term, seq_rows)
    qkv = (qkv_sum + bias_rows).astype(jnp.bfloat16)
    blocks = qkv.reshape(seq_count, LEN, 3, width_col)
    attn_blocks, log_totals = lax.map(attend_forward, (blocks, prefix))
    attn = attn_blocks.reshape(seq_rows, width_col)
    attn_gathered = row_rows(attn)

    def out_term(first_row, row_count):
        return jnp.dot(attn_gathered, w_out, preferred_element_type=jnp.float32)

    middle = (
        residual
        + summed_over_col(out_term, local_rows)
        + take_portion(out_bias, row_place, width_row, 0)
    )
    grad_output = cotangent_local.astype(jnp.float32)
    second_gain = take_portion(ln2_gain, row_place, width_row, 0)
    second_normed, second_unit, second_inverse = norm_forward(
        middle, second_gain, take_portion(ln2_bias, row_place, width_row, 0), feature_totals
    )
    second_gathered = column_rows(second_normed.astype(jnp.bfloat16))

    def up_term(first_row, row_count):
        return jnp.dot(second_gathered, w_fc, preferred_element_type=jnp.float32)

    hidden = summed_over_row(up_term, seq_rows) + take_portion(fc_bias, col_place, hidden_col, 0)
    active, gelu_pull = jax.vjp(gelu_tanh, hidden)
    active_gathered = row_rows(active.astype(jnp.bfloat16))

    def down_term(first_row, row_count):
        return jnp.einsum("tf,df->td", active_gathered, w_proj, preferred_element_type=jnp.float32)

    final_rows = (
        middle
        + summed_over_col(down_term, local_rows)
        + take_portion(proj_bias, row_place, width_row, 0)
    )
    output = final_rows.astype(jnp.bfloat16)
    grad_gathered = column_rows(cotangent_local)
    w_proj_grad = jnp.einsum(
        "tf,td->df", active_gathered, grad_gathered, preferred_element_type=jnp.float32
    )

    def active_term(first_row, row_count):
        return jnp.einsum("td,df->tf", grad_gathered, w_proj, preferred_element_type=jnp.float32)

    hidden_grad = gelu_pull(summed_over_row(active_term, seq_rows))[0].astype(jnp.bfloat16)
    hidden_gathered = row_rows(hidden_grad)
    w_fc_grad = jnp.einsum(
        "td,tf->df", second_gathered, hidden_gathered, preferred_element_type=jnp.float32
    )

    def second_term(first_row, row_count):
        return jnp.einsum("tf,df->td", hidden_gathered, w_fc, preferred_element_type=jnp.float32)

    second_grad = summed_over_col(second_term, local_rows)
    middle_grad = grad_output + norm_backward(
        second_grad, second_unit, second_inverse, second_gain, feature_totals
    )
    ln2_gain_part = place_portion(jnp.sum(second_grad * second_unit, axis=0), row_place, D, 0)
    ln2_bias_part = place_portion(jnp.sum(second_grad, axis=0), row_place, D, 0)
    fc_bias_part = place_portion(jnp.sum(hidden_grad.astype(jnp.float32), axis=0), col_place, FF, 0)
    proj_bias_part = place_portion(jnp.sum(grad_output, axis=0), row_place, D, 0)
    branch_grad = middle_grad.astype(jnp.bfloat16)
    branch_gathered = column_rows(branch_grad)
    w_out_grad = jnp.einsum(
        "te,td->ed", attn_gathered, branch_gathered, preferred_element_type=jnp.float32
    )

    def attn_term(first_row, row_count):
        return jnp.einsum("td,ed->te", branch_gathered, w_out, preferred_element_type=jnp.float32)

    attn_grad = summed_over_row(attn_term, seq_rows).astype(jnp.bfloat16)
    qkv_grad = lax.map(
        attend_backward, (blocks, prefix, log_totals, attn_grad.reshape(seq_count, LEN, width_col))
    )
    qkv_grad = qkv_grad.reshape(seq_rows, 3, width_col)
    qkv_gathered = row_rows(qkv_grad)
    w_qkv_grad = jnp.einsum(
        "td,tse->sde", first_gathered, qkv_gathered, preferred_element_type=jnp.float32
    )

    def first_term(first_row, row_count):
        return jnp.einsum("tse,sde->td", qkv_gathered, w_qkv, preferred_element_type=jnp.float32)

    first_grad = summed_over_col(first_term, local_rows)
    input_grad = middle_grad + norm_backward(
        first_grad, first_unit, first_inverse, first_gain, feature_totals
    )
    qkv_totals = jnp.sum(qkv_grad.astype(jnp.float32), axis=0)
    qv_part = place_portion(jnp.stack([qkv_totals[0], qkv_totals[2]]), col_place, D, 1)
    out_bias_part = place_portion(jnp.sum(branch_grad.astype(jnp.float32), axis=0), row_place, D, 0)
    ln1_gain_part = place_portion(jnp.sum(first_grad * first_unit, axis=0), row_place, D, 0)
    ln1_bias_part = place_portion(jnp.sum(first_grad, axis=0), row_place, D, 0)
    vectors = lax.psum(
        (
            ln1_gain_part,
            ln1_bias_part,
            qv_part,
            out_bias_part,
            ln2_gain_part,
            ln2_bias_part,
            fc_bias_part,
            proj_bias_part,
        ),
        ("dp", "row", "col"),
    )
    matrices = (
        lax.psum(w_qkv_grad.astype(jnp.bfloat16), "dp").astype(jnp.float32),
        lax.psum(w_out_grad.astype(jnp.bfloat16), "dp").astype(jnp.float32),
        lax.psum(w_fc_grad.astype(jnp.bfloat16), "dp").astype(jnp.float32),
        lax.psum(w_proj_grad.astype(jnp.bfloat16), "dp").astype(jnp.float32),
    )
    return (
        output.T,
        input_grad.T,
        vectors[0],
        vectors[1],
        matrices[0],
        vectors[2],
        matrices[1],
        vectors[3],
        vectors[4],
        vectors[5],
        matrices[2],
        vectors[6],
        matrices[3],
        vectors[7],
    )


def solution(mesh):
    placed = (
        P("row", ("dp", "col")),
        P(("dp", "row")),
        P(),
        P(),
        P(None, "row", "col"),
        P(),
        P("col", "row"),
        P(),
        P(),
        P(),
        P("row", "col"),
        P(),
        P("row", "col"),
        P(),
        P("row", ("dp", "col")),
    )
    return jax.shard_map(
        on_device,
        mesh=mesh,
        in_specs=placed,
        out_specs=(
            P("row", ("dp", "col")),
            P("row", ("dp", "col")),
            P(),
            P(),
            P(None, "row", "col"),
            P(),
            P("col", "row"),
            P(),
            P(),
            P(),
            P("row", "col"),
            P(),
            P("row", "col"),
            P(),
        ),
        check_vma=False,
    )
```

profile of v0, /device:TPU:0, one launch (start us, length us, event | category | flops | bytes accessed | tf_op | source)
XLA Modules:
  0.0 1165.3 jit_solution(17599242956197801233)
XLA Ops:
  11.0 11.5 all-reduce.4
  22.5 1.9 fusion.38
  25.6 35.4 %all-gather.9.cloned.1.call-done = bf16[4096,192]{0,1:T(8,128)(2,1)} async-done(((bf16[1024,192]{0,1:T(8,128)(2,1)}), bf16[4096,192]{0,1:T(8,128)(2,1)}) %all-gather.9.cloned.1.call-update) | async-done | bytes 1572880 | tf_op jit(solution)/shard_map/all_gather | solution.py:21
  61.1 6.4 fusion.61
  69.5 92.0 %reduce-scatter.9.cloned.1.call-done = f32[1024,3,192]{0,2,1:T(8,128)} async-done(((f32[4096,3,192]{0,2,1:T(8,128)}), f32[1024,3,192]{0,2,1:T(8,128)}) %reduce-scatter.9.cloned.1.call-update) | async-done | bytes 2359312 | tf_op jit(solution)/shard_map/reduce_scatter | solution.py:29
  161.5 1.9 add_convert_fusion
  163.5 3.2 fusion.55
  168.5 2.8 copy-done.2
  171.3 3.0 fusion.21
  174.4 31.1 %all-gather.11.cloned.1.call-done = bf16[4096,192]{0,1:T(8,128)(2,1)} async-done(((bf16[1024,192]{0,1:T(8,128)(2,1)}), bf16[4096,192]{0,1:T(8,128)(2,1)}) %all-gather.11.cloned.1.call-update) | async-done | bytes 1572880 | tf_op jit(solution)/shard_map/all_gather | solution.py:25
  205.5 3.7 fusion.56
  212.1 57.5 %reduce-scatter.11.cloned.1.call-done = f32[1024,192]{0,1:T(8,128)} async-done(((f32[4096,192]{0,1:T(8,128)}), f32[1024,192]{0,1:T(8,128)}) %reduce-scatter.11.cloned.1.call-update) | async-done | bytes 786448 | tf_op jit(solution)/shard_map/reduce_scatter | solution.py:38
  270.9 10.1 all-reduce.3
  282.1 26.1 %all-gather.17.cloned.1.call-done = bf16[4096,192]{0,1:T(8,128)(2,1)} async-done(((bf16[1024,192]{0,1:T(8,128)(2,1)}), bf16[4096,192]{0,1:T(8,128)(2,1)}) %all-gather.17.cloned.1.call-update) | async-done | bytes 1572880 | tf_op jit(solution)/shard_map/all_gather | solution.py:21
  308.2 7.7 fusion.59
  316.2 30.0 %all-gather.13.cloned.1.call-done = bf16[4096,192]{0,1:T(8,128)(2,1)} async-done(((bf16[1024,192]{0,1:T(8,128)(2,1)}), bf16[4096,192]{0,1:T(8,128)(2,1)}) %all-gather.13.cloned.1.call-update) | async-done | bytes 1572880 | tf_op jit(solution)/shard_map/all_gather | solution.py:21
  346.2 7.9 fusion.57
  354.9 114.0 %reduce-scatter.17.cloned.1.call-done = f32[1024,768]{1,0:T(8,128)} async-done(((f32[4096,768]{1,0:T(8,128)}), f32[1024,768]{1,0:T(8,128)}) %reduce-scatter.17.cloned.1.call-update) | async-done | bytes 3145744 | tf_op jit(solution)/shard_map/reduce_scatter | solution.py:29
  468.9 123.9 %reduce-scatter.13.cloned.1.call-done = f32[1024,768]{1,0:T(8,128)} async-done(((f32[4096,768]{1,0:T(8,128)}), f32[1024,768]{1,0:T(8,128)}) %reduce-scatter.13.cloned.1.call-update) | async-done | bytes 3145744 | tf_op jit(solution)/shard_map/reduce_scatter | solution.py:29
  592.7 5.6 convert_reduce_fusion
  598.5 70.2 %all-gather.19.cloned.1.call-done = bf16[4096,768]{1,0:T(8,128)(2,1)} async-done(((bf16[1024,768]{1,0:T(8,128)(2,1)}), bf16[4096,768]{1,0:T(8,128)(2,1)}) %all-gather.19.cloned.1.call-update) | async-done | bytes 6291472 | tf_op jit(solution)/shard_map/all_gather | solution.py:25
  668.7 6.6 fusion.60
  675.4 60.4 %reduce-scatter.19.cloned.1.call-done = f32[1024,192]{0,1:T(8,128)} async-done(((f32[4096,192]{0,1:T(8,128)}), f32[1024,192]{0,1:T(8,128)}) %reduce-scatter.19.cloned.1.call-update) | async-done | bytes 786448 | tf_op jit(solution)/shard_map/reduce_scatter | solution.py:38
  737.3 10.1 all-reduce.2
  747.3 2.2 convert_reduce_fusion.4
  749.7 35.4 %all-gather.21.cloned.1.call-done = bf16[4096,192]{0,1:T(8,128)(2,1)} async-done(((bf16[1024,192]{0,1:T(8,128)(2,1)}), bf16[4096,192]{0,1:T(8,128)(2,1)}) %all-gather.21.cloned.1.call-update) | async-done | bytes 1572880 | tf_op jit(solution)/shard_map/all_gather | solution.py:21
  785.0 3.7 fusion.62
  789.8 41.9 %reduce-scatter.21.cloned.1.call-done = f32[1024,192]{0,1:T(8,128)} async-done(((f32[4096,192]{0,1:T(8,128)}), f32[1024,192]{0,1:T(8,128)}) %reduce-scatter.21.cloned.1.call-update) | async-done | bytes 786448 | tf_op jit(solution)/shard_map/reduce_scatter | solution.py:29
  833.0 6.1 multiply_reduce_fusion
  841.8 5.2 multiply_convert_fusion
  847.0 4.2 fusion.16
  851.6 2.0 fusion.17
  853.7 2.1 fusion.18
  857.6 4.9 convolution_convert_fusion.1
  862.4 41.3 %all-gather.15.cloned.1.call-done = bf16[4096,768]{1,0:T(8,128)(2,1)} async-done(((bf16[1024,768]{1,0:T(8,128)(2,1)}), bf16[4096,768]{1,0:T(8,128)(2,1)}) %all-gather.15.cloned.1.call-update) | async-done | bytes 6291472 | tf_op jit(solution)/shard_map/all_gather | solution.py:25
  903.8 5.5 fusion.25
  910.5 52.1 %all-gather.23.cloned.1.call-done = bf16[4096,3,192]{0,2,1:T(8,128)(2,1)} async-done(((bf16[1024,3,192]{0,2,1:T(8,128)(2,1)}), bf16[4096,3,192]{0,2,1:T(8,128)(2,1)}) %all-gather.23.cloned.1.call-update) | async-done | bytes 4718608 | tf_op jit(solution)/shard_map/all_gather | solution.py:25
  962.6 5.0 fusion.26
  967.9 5.4 convolution_bitcast_fusion
  974.3 6.8 fusion.58
  983.0 4.3 all-reduce.8.cloned.1.call-done
  987.3 1.8 convert_element_type.122
  990.9 1.9 copy.34
  994.5 56.6 %reduce-scatter.23.cloned.1.call-done = f32[1024,192]{0,1:T(8,128)} async-done(((f32[4096,192]{0,1:T(8,128)}), f32[1024,192]{0,1:T(8,128)}) %reduce-scatter.23.cloned.1.call-update) | async-done | bytes 786448 | tf_op jit(solution)/shard_map/reduce_scatter | solution.py:38
  1052.5 10.1 all-reduce.1
  1062.7 51.0 %reduce-scatter.15.cloned.1.call-done = f32[1024,192]{0,1:T(8,128)} async-done(((f32[4096,192]{0,1:T(8,128)}), f32[1024,192]{0,1:T(8,128)}) %reduce-scatter.15.cloned.1.call-update) | async-done | bytes 786448 | tf_op jit(solution)/shard_map/reduce_scatter | solution.py:38
  1113.6 2.9 fusion.43
  1117.1 41.7 %all-reduce = (f32[768]{0:T(1024)}, f32[768]{0:T(1024)}, f32[2,768]{1,0:T(2,128)}, f32[768]{0:T(1024)}, f32[768]{0:T(1024)}, /*index=5*/f32[768]{0:T(1024)}, f32[3072]{0:T(1024)}, f32[768]{0:T(1024)}) all-reduce(f32[768]{0:T(1024)S(1)} %dynamic_update_slice.33, ...), channel_id=1, replica_groups=mesh['dp'=2,'row'=4,'col'=4] {'dp','row','col'}, use_global_device_ids=true, to_apply=%region_28.29 | all-reduce | flops 9216 | bytes 73728 | tf_op jit(solution)/shard_map/psum | solution.py:266
  (126 shorter events, 33.4 us)
Async XLA Ops:
  7.2 339.0 %copy-start = (bf16[192,768]{1,0:T(8,128)(2,1)S(1)}, bf16[192,768]{1,0:T(8,128)(2,1)}, u32[]{:S(2)}) copy-start(bf16[192,768]{1,0:T(8,128)(2,1)} %param.25) | copy-start | bytes 884740
  7.2 53.9 %all-gather.9.cloned.1.call-start = ((), (), s32[]{:S(2)}) async-start(), calls=%async_computation.8 | async-start | bytes 1966080 | tf_op jit(solution)/shard_map/all_gather | solution.py:21
  24.4 137.1 %reduce-scatter.9.cloned.1.call-start = ((), (), s32[]{:S(2)}) async-start(), calls=%async_computation.9 | async-start | bytes 11796480 | tf_op jit(solution)/shard_map/reduce_scatter | solution.py:29
  67.5 137.9 %all-gather.11.cloned.1.call-start = ((), (), s32[]{:S(2)}) async-start(), calls=%async_computation.10 | async-start | bytes 1966080 | tf_op jit(solution)/shard_map/all_gather | solution.py:25
  163.5 3.3 copy-start.8
  163.5 5.0 copy-start.11
  166.7 4.6 copy-start.2
  171.3 34.1 %copy-start.17 = (bf16[192,192]{1,0:T(8,128)(2,1)S(1)}, bf16[192,192]{1,0:T(8,128)(2,1)}, u32[]{:S(2)}) copy-start(bf16[192,192]{1,0:T(8,128)(2,1)} %param.21) | copy-start | bytes 221188
  174.3 95.3 %reduce-scatter.11.cloned.1.call-start = ((), (), s32[]{:S(2)}) async-start(), calls=%async_computation.11 | async-start | bytes 3932160 | tf_op jit(solution)/shard_map/reduce_scatter | solution.py:38
  209.2 60.4 %copy-start.4 = (bf16[192,1024]{1,0:T(8,128)(2,1)S(1)}, bf16[192,1024]{1,0:T(8,128)(2,1)}, u32[]{:S(2)}) copy-start(bf16[192,1024]{1,0:T(8,128)(2,1)} %param.15) | copy-start | bytes 1179652
  209.2 99.0 %copy-start.15 = (bf16[192,768]{1,0:T(8,128)(2,1)S(1)}, bf16[192,768]{1,0:T(8,128)(2,1)}, u32[]{:S(2)}) copy-start(bf16[192,768]{1,0:T(8,128)(2,1)} %param.27) | copy-start | bytes 884740
  209.2 99.0 %all-gather.17.cloned.1.call-start = ((), (), s32[]{:S(2)}) async-start(), calls=%async_computation.16 | async-start | bytes 1966080 | tf_op jit(solution)/shard_map/all_gather | solution.py:21
  209.8 136.4 %all-gather.13.cloned.1.call-start = ((), (), s32[]{:S(2)}) async-start(), calls=%async_computation.12 | async-start | bytes 1966080 | tf_op jit(solution)/shard_map/all_gather | solution.py:21
  282.0 186.9 %reduce-scatter.17.cloned.1.call-start = ((), (), s32[]{:S(2)}) async-start(), calls=%async_computation.17 | async-start | bytes 15728640 | tf_op jit(solution)/shard_map/reduce_scatter | solution.py:29
  315.9 276.8 %reduce-scatter.13.cloned.1.call-start = ((), (), s32[]{:S(2)}) async-start(), calls=%async_computation.13 | async-start | bytes 15728640 | tf_op jit(solution)/shard_map/reduce_scatter | solution.py:29
  354.0 314.7 %all-gather.19.cloned.1.call-start = ((), (), s32[]{:S(2)}) async-start(), calls=%async_computation.18 | async-start | bytes 7864320 | tf_op jit(solution)/shard_map/all_gather | solution.py:25
  598.4 137.4 %reduce-scatter.19.cloned.1.call-start = ((), (), s32[]{:S(2)}) async-start(), calls=%async_computation.19 | async-start | bytes 3932160 | tf_op jit(solution)/shard_map/reduce_scatter | solution.py:38
  675.3 72.0 %copy-start.7 = (bf16[192,1024]{1,0:T(8,128)(2,1)S(1)}, bf16[192,1024]{1,0:T(8,128)(2,1)}, u32[]{:S(2)}) copy-start(bf16[192,1024]{1,0:T(8,128)(2,1)} %param.29) | copy-start | bytes 1179652
  675.4 109.6 %all-gather.21.cloned.1.call-start = ((), (), s32[]{:S(2)}) async-start(), calls=%async_computation.20 | async-start | bytes 1966080 | tf_op jit(solution)/shard_map/all_gather | solution.py:21
  749.6 82.1 %reduce-scatter.21.cloned.1.call-start = ((), (), s32[]{:S(2)}) async-start(), calls=%async_computation.21 | async-start | bytes 3932160 | tf_op jit(solution)/shard_map/reduce_scatter | solution.py:29
  788.7 44.2 %copy-start.12 = (bf16[1024,1,192]{0,2,1:T(8,128)(2,1)S(1)}, bf16[1024,1,192]{0,2,1:T(8,128)(2,1)}, u32[]{:S(2)}) copy-start(bf16[1024,1,192]{0,2,1:T(8,128)(2,1)} %copy-done.11) | copy-start | bytes 1179652
  788.8 115.0 %all-gather.15.cloned.1.call-start = ((), (), s32[]{:S(2)}) async-start(), calls=%async_computation.14 | async-start | bytes 7864320 | tf_op jit(solution)/shard_map/all_gather | solution.py:25
  789.5 173.0 %all-gather.23.cloned.1.call-start = ((), (), s32[]{:S(2)}) async-start(), calls=%async_computation.22 | async-start | bytes 5898240 | tf_op jit(solution)/shard_map/all_gather | solution.py:25
  832.9 6.2 slice-start
  832.9 7.1 slice-start.1
  833.0 8.8 slice-start.2
  841.8 5.2 copy-start.9
  847.0 4.6 copy-start.3
  855.7 1.8 copy-start.10
  857.0 130.3 %all-reduce.8.cloned.1.call-start = ((), (), s32[]{:S(2)}) async-start(), calls=%async_computation.24 | async-start | bytes 1966080 | tf_op jit(solution)/shard_map/psum | solution.py:280
  862.4 46.8 %copy-start.6 = (bf16[4096,192]{0,1:T(8,128)(2,1)S(1)}, bf16[4096,192]{0,1:T(8,128)(2,1)}, u32[]{:S(2)}) copy-start(bf16[4096,192]{0,1:T(8,128)(2,1)} %all-gather.11.cloned.1.call-done) | copy-start | bytes 4718596
  903.8 5.5 copy-start.13
  910.5 57.4 %copy-start.14 = (bf16[3,192,192]{2,1,0:T(8,128)(2,1)S(1)}, bf16[3,192,192]{2,1,0:T(8,128)(2,1)}, u32[]{:S(2)}) copy-start(bf16[3,192,192]{2,1,0:T(8,128)(2,1)} %param.19) | copy-start | bytes 663556
  967.5 83.5 %reduce-scatter.23.cloned.1.call-start = ((), (), s32[]{:S(2)}) async-start(), calls=%async_computation.23 | async-start | bytes 3932160 | tf_op jit(solution)/shard_map/reduce_scatter | solution.py:38
  973.3 1.0 copy-start.16
  973.3 140.3 %reduce-scatter.15.cloned.1.call-start = ((), (), s32[]{:S(2)}) async-start(), calls=%async_computation.15 | async-start | bytes 3932160 | tf_op jit(solution)/shard_map/reduce_scatter | solution.py:38
  981.1 132.5 %copy-start.5 = (f32[1024,192]{0,1:T(8,128)S(1)}, f32[1024,192]{0,1:T(8,128)}, u32[]{:S(2)}) copy-start(f32[1024,192]{0,1:T(8,128)} %reduce-scatter.19.cloned.1.call-done) | copy-start | bytes 2359300
  992.8 165.9 %copy-start.1 = (bf16[192,768]{1,0:T(8,128)(2,1)S(1)}, bf16[192,768]{1,0:T(8,128)(2,1)}, u32[]{:S(2)}) copy-start(bf16[192,768]{1,0:T(8,128)(2,1)} %param.25) | copy-start | bytes 884740
Sparse Core Ops, SparseCore 0:
  24.6 36.4 all-gather.8
  67.6 93.8 reduce-scatter.8
  174.4 30.9 all-gather.10
  209.3 60.2 reduce-scatter.10
  271.0 37.1 all-gather.16
  310.2 35.9 all-gather.12
  349.3 119.5 reduce-scatter.16
  472.0 120.7 reduce-scatter.12
  598.5 70.1 all-gather.18
  675.5 60.2 reduce-scatter.18
  749.7 35.2 all-gather.20
  788.9 42.8 reduce-scatter.20
  833.6 70.1 all-gather.14
  905.5 57.0 all-gather.22
  967.7 19.5 all-reduce.7
  989.5 61.4 reduce-scatter.22
  1053.3 60.2 reduce-scatter.14
where the time goes:
time: 1170 us
  waiting for transfers between devices  924 us (79%)
  matrix products  85.4 us (7%)
  blocking collectives  83.4 us (7%)
  other arithmetic  37.2 us (3%)
  local copies, waits for them, and re-layouts  18.6 us (2%)
  between operations  15 us (1%)
    reduce_scatter x4, waiting for transfers between devices, summed_over_row(): lax.psum_scatter(term_fn(jnp.int32(0), row_count * lax.axis_size('row')),...  372 us
    reduce_scatter x4, waiting for transfers between devices, summed_over_col(): lax.psum_scatter(term_fn(jnp.int32(0), row_count * lax.axis_size('col')),...  225 us
    all_gather x4, waiting for transfers between devices, row_rows(): return lax.all_gather(values, 'row', axis=0, tiled=True)  195 us
    all_gather x4, waiting for transfers between devices, column_rows(): return lax.all_gather(values, 'col', axis=0, tiled=True)  127 us
    psum x4, blocking collectives, feature_totals(): return lax.psum(values, 'row')  41.7 us
    psum x1, blocking collectives, on_device(): lax.psum((ln1_gain_part, ln1_bias_part, qv_part, out_bias_part, ln2_gain_...  41.7 us
  transfers between devices with their start and end apart: 17, of which 17 were waited for; matrix products, arithmetic and copies ran while one was open for 7% of the time, Pallas kernels for 0%

commit v1 on v0

--- a/solution.py
+++ b/solution.py
@@ -1,6 +1,10 @@
+import functools
+
 import jax
 import jax.numpy as jnp
 from jax import lax
+from jax.experimental import pallas as pl
+from jax.experimental.pallas import tpu as pltpu
 from jax.sharding import PartitionSpec as P
 
 D = 768
@@ -130,7 +134,7 @@
     return stacked.astype(jnp.bfloat16)
 
 
-def on_device(
+def general_device(
     tokens,
     prefix,
     ln1_gain,
@@ -300,7 +304,742 @@
     )
 
 
+MESH = pl.DeviceIdType.MESH
+WIDTH = 192
+HALF = 96
+QUARTER = 256
+LANES = 128
+WQ = 3 * WIDTH
+VMEM_LIMIT = 67043328
+REMOTES = 112
+LOCALS = 40
+FACTOR = HEAD_DIM ** (-0.5)
+ANY = pl.BlockSpec(memory_space=pl.ANY)
+GAIN1, BIAS1, OUT_BIAS, GAIN2, BIAS2, FC_BIAS, QKV_BIAS, PROJ_BIAS = range(8)
+V_GAIN1, V_BIAS1, V_QUERY, V_VALUE, V_OUT, V_GAIN2, V_BIAS2, V_PROJ, V_FC = range(9)
+CENTER, INVERSE = range(2)
+
+
+def dot(left, right, left_axis, right_axis):
+    return lax.dot_general(
+        left, right, (((left_axis,), (right_axis,)), ((), ())), preferred_element_type=jnp.float32
+    )
+
+
+def low(value):
+    return value.astype(jnp.bfloat16)
+
+
+def wide(value):
+    return value.astype(jnp.float32)
+
+
+def aligned(start, size):
+    return pl.ds(pl.multiple_of(start, size), size)
+
+
+def merged(value):
+    return value.reshape((value.shape[0] * value.shape[1],) + value.shape[2:])
+
+
+def each(count, body):
+    def step(i, carry):
+        body(i)
+        return carry
+
+    lax.fori_loop(0, count, step, 0)
+
+
+class Links:
+    def __init__(self, send_sems, recv_sems, local_sems):
+        self.d, self.r, self.c = (lax.axis_index(n) for n in ("dp", "row", "col"))
+        self.send_sems, self.recv_sems, self.local_sems = send_sems, recv_sems, local_sems
+        self.remotes = 0
+        self.locals = 0
+
+    def across(self, k):
+        if k == 0:
+            return self.r
+        if k == 1:
+            return self.r + 1 - 2 * lax.rem(self.r, 2)
+        return lax.rem(self.r + 2, 4) if k == 2 else 3 - self.r
+
+    def plane(self, k):
+        return (self.d, self.across(k), self.c)
+
+    def height(self, k):
+        return lax.rem(self.c + k, 4)
+
+    def column(self, k):
+        return (self.d, self.r, self.height(k))
+
+    def partner(self):
+        return (1 - self.d, self.r, self.c)
+
+    def half(self, mine=True):
+        place = self.d if mine else 1 - self.d
+        return pl.ds(pl.multiple_of(place * HALF, 16), HALF)
+
+    def meet(self, *devices):
+        barrier = pltpu.get_barrier_semaphore()
+        for device in devices:
+            pl.semaphore_signal(barrier, 1, device_id=device, device_id_type=MESH)
+        pl.semaphore_wait(barrier, len(devices))
+
+    def send(self, source, target, device):
+        place = self.remotes
+        self.remotes += 1
+        copy = pltpu.make_async_remote_copy(
+            src_ref=source,
+            dst_ref=target,
+            send_sem=self.send_sems.at[place],
+            recv_sem=self.recv_sems.at[place],
+            device_id=device,
+            device_id_type=MESH,
+        )
+        copy.start()
+        return copy
+
+    def local(self, source, target):
+        place = self.locals
+        self.locals += 1
+        copy = pltpu.make_async_copy(source, target, self.local_sems.at[place])
+        copy.start()
+        return copy
+
+
+class PlaneGather:
+    def __init__(self, links, target):
+        self.links, self.target = links, target
+        rows = target.shape[1] // 2
+        self.low, self.high = pl.ds(0, rows), pl.ds(rows, rows)
+        first, second = target.at[links.r, self.low], target.at[links.r, self.high]
+        self.x_low = links.send(first, first, links.plane(1))
+        self.y_high = links.send(second, second, links.plane(2))
+        self.x_high = links.send(second, second, links.plane(1))
+        self.y_low = links.send(first, first, links.plane(2))
+
+    def relay(self):
+        links = self.links
+        self.x_low.wait_recv()
+        block = self.target.at[links.across(1), self.low]
+        self.on_y = links.send(block, block, links.plane(2))
+        self.y_high.wait_recv()
+        block = self.target.at[links.across(2), self.high]
+        self.on_x = links.send(block, block, links.plane(1))
+
+    def finish(self):
+        self.x_high.wait_recv()
+        self.y_low.wait_recv()
+        for copy in (self.x_low, self.y_high, self.x_high, self.y_low):
+            copy.wait_send()
+        self.on_y.wait()
+        self.on_x.wait()
+
+
+class WeightGather:
+    def __init__(self, links, stage, target):
+        self.links, self.stage, self.target = links, stage, target
+        block = stage.at[links.c]
+        self.rising = [links.send(block, block, links.column(k)) for k in (2, 1, 3)]
+
+    def cross(self):
+        links, mine = self.links, self.links.half()
+        for copy in self.rising:
+            copy.wait()
+        self.crossing = [
+            links.send(self.stage.at[links.across(k)], self.target.at[links.r, mine], links.plane(k))
+            for k in (3, 1, 2)
+        ]
+        self.crossing.append(links.local(self.stage.at[links.r], self.target.at[links.r, mine]))
+
+    def share(self):
+        for copy in self.crossing:
+            copy.wait()
+        block = self.target.at[:, self.links.half()]
+        self.shared = self.links.send(block, block, self.links.partner())
+
+    def finish(self):
+        self.shared.wait()
+
+
+class SquareGather(WeightGather):
+    def cross(self):
+        links, mine = self.links, self.links.half()
+        for copy in self.rising:
+            copy.wait()
+        block = self.target.at[links.r, :, mine]
+        self.crossing = [links.send(self.stage, block, links.plane(k)) for k in (3, 1, 2)]
+        self.crossing.append(links.local(self.stage, block))
+
+    def share(self):
+        for copy in self.crossing:
+            copy.wait()
+        block = self.target.at[:, :, self.links.half()]
+        self.shared = self.links.send(block, block, self.links.partner())
+
+
+def add_rows(target, terms):
+    def step(i):
+        place = aligned(i * 16, 16)
+        total = wide(terms[0][place, :])
+        for term in terms[1:]:
+            total = total + wide(term[place, :])
+        target[place, :] = total.astype(target.dtype)
+
+    each(target.shape[0] // 16, step)
+
+
+class WeightReduce:
+    def __init__(self, links, grad, near, sums, cross, high, final, result):
+        self.links, self.grad, self.near, self.sums = links, grad, near, sums
+        self.crossed, self.high, self.final, self.result = cross, high, final, result
+        self.to_near = links.send(grad.at[:, links.half(False)], near, links.partner())
+
+    def cross(self):
+        links, mine = self.links, self.links.half()
+        self.to_near.wait()
+        for b in range(4):
+            add_rows(self.sums.at[b], [self.grad.at[b, mine], self.near.at[b]])
+        self.crossing = [
+            links.send(self.sums.at[links.across(k)], self.crossed.at[links.r], links.plane(k))
+            for k in (3, 1, 2)
+        ]
+        self.crossing.append(links.local(self.sums.at[links.r], self.crossed.at[links.r]))
+
+    def rise(self):
+        links = self.links
+        for copy in self.crossing:
+            copy.wait()
+        self.rising = [
+            links.send(self.crossed.at[links.height(k)], self.high.at[k - 1], links.column(k))
+            for k in (2, 1, 3)
+        ]
+
+    def total(self):
+        links, mine = self.links, self.links.half()
+        for copy in self.rising:
+            copy.wait()
+        high = self.high
+        add_rows(self.final, [self.crossed.at[links.c], high.at[0], high.at[1], high.at[2]])
+        self.last = [
+            links.send(self.final, self.result.at[mine], links.partner()),
+            links.local(self.final, self.result.at[mine]),
+        ]
+
+    def finish(self):
+        for copy in self.last:
+            copy.wait()
+
+
+class SquareReduce(WeightReduce):
+    def __init__(self, links, grad, near, sums, came, cross, high, final, result):
+        self.came = came
+        self.links, self.grad, self.near, self.sums = links, grad, near, sums
+        self.crossed, self.high, self.final, self.result = cross, high, final, result
+        self.to_near = links.send(grad.at[:, :, links.half(False)], near, links.partner())
+
+    def cross(self):
+        links, mine = self.links, self.links.half()
+        self.to_near.wait()
+
+        def add(i):
+            b, e = lax.div(i, 4), lax.rem(i, 4)
+            add_rows(self.sums.at[b, e], [self.grad.at[b, e, mine], self.near.at[b, e]])
+
+        each(16, add)
+        self.crossing = [
+            links.send(self.sums.at[links.across(k)], self.came.at[k - 1], links.plane(k))
+            for k in (3, 1, 2)
+        ]
+
+    def rise(self):
+        for copy in self.crossing:
+            copy.wait()
+
+        def add(e):
+            terms = [self.sums.at[self.links.r, e]] + [self.came.at[k, e] for k in range(3)]
+            add_rows(self.crossed.at[e], terms)
+
+        each(4, add)
+        self.crossing = []
+        WeightReduce.rise(self)
+
+
+def normalize(source_of, target, stats, gain, offset):
+    def step(j):
+        lanes = aligned(j * LANES, LANES)
+        values = source_of(lanes)
+        center = jnp.sum(values, axis=0, keepdims=True) / D
+        square = jnp.sum(values * values, axis=0, keepdims=True) / D
+        inverse = lax.rsqrt(square - center * center + epsilon)
+        stats[CENTER : CENTER + 1, lanes] = center
+        stats[INVERSE : INVERSE + 1, lanes] = inverse
+        target[:, lanes] = low((values - center) * inverse * gain[...] + offset[...])
+
+    each(LEN // LANES, step)
+
+
+def key_span(block):
+    return max(512, (block + 1) * QUARTER), block * QUARTER
+
+
+def visible(block, first, last, limit_value):
+    shape = (last - first, QUARTER)
+    keys = lax.broadcasted_iota(jnp.int32, shape, 0) + first
+    queries = lax.broadcasted_iota(jnp.int32, shape, 1) + block * QUARTER
+    return (keys <= queries) | (keys < limit_value)
+
+
+def masked(value, block, limit_value, fill):
+    last, first = key_span(block)
+    tail = jnp.where(visible(block, first, last, limit_value), value[first:], fill)
+    return jnp.concatenate([value[:first], tail], axis=0) if first else tail
+
+
+def head_rows(h, part):
+    return pl.ds(pl.multiple_of(h * HEAD_DIM + part * WIDTH, HEAD_DIM), HEAD_DIM)
+
+
+def attend(qkv, limit_value, attn_of, log_total):
+    def head(h):
+        for block in range(4):
+            last, _ = key_span(block)
+            lanes = slice(block * QUARTER, (block + 1) * QUARTER)
+            queries = qkv[head_rows(h, 0), lanes] * jnp.bfloat16(FACTOR)
+            scores = dot(qkv[head_rows(h, 1), :last], queries, 0, 0)
+            scores = masked(scores, block, limit_value, masked_score)
+            largest = jnp.max(scores, axis=0, keepdims=True)
+            weights = jnp.exp(scores - largest)
+            total = jnp.sum(weights, axis=0, keepdims=True)
+            mixed = dot(qkv[head_rows(h, 2), :last], low(weights), 1, 0)
+            attn_of(head_rows(h, 0), lanes, low(mixed * (1.0 / total)))
+            log_total[pl.ds(h, 1), lanes] = largest + jnp.log(total)
+
+    each(3, head)
+
+
+def attend_back(qkv, limit_value, attn_of, log_total, out_grad, qkv_grad, key_sum, value_sum):
+    def head(h):
+        for block in (3, 2, 1, 0):
+            last, _ = key_span(block)
+            lanes = slice(block * QUARTER, (block + 1) * QUARTER)
+            queries = qkv[head_rows(h, 0), lanes] * jnp.bfloat16(FACTOR)
+            grads = out_grad[head_rows(h, 0), lanes]
+            inner = jnp.sum(
+                wide(attn_of(head_rows(h, 0), lanes)) * wide(grads), axis=0, keepdims=True
+            )
+            scores = dot(qkv[head_rows(h, 1), :last], queries, 0, 0)
+            probs = jnp.exp(scores - log_total[pl.ds(h, 1), lanes])
+            probs = masked(probs, block, limit_value, 0.0)
+            weight_grad = dot(qkv[head_rows(h, 2), :last], grads, 0, 0)
+            score_grad = low(probs * (weight_grad - inner))
+            query_grad = dot(qkv[head_rows(h, 1), :last], score_grad, 1, 0) * FACTOR
+            qkv_grad[head_rows(h, 0), lanes] = low(query_grad)
+            key_grad = dot(queries, score_grad, 1, 1)
+            value_grad = dot(grads, low(probs), 1, 1)
+            if block == 3:
+                key_sum[...] = key_grad
+                value_sum[...] = value_grad
+            else:
+                key_sum[:, :last] += key_grad
+                value_sum[:, :last] += value_grad
+        qkv_grad[head_rows(h, 1), :] = low(key_sum[...])
+        qkv_grad[head_rows(h, 2), :] = low(value_sum[...])
+
+    each(3, head)
+
+
+def gelu_parts(u):
+    slope = (2.0 / 3.141592653589793) ** 0.5
+    square = u * u
+    bent = jnp.tanh(slope * u * (1.0 + 0.044715 * square))
+    shared = 0.5 * (1.0 + bent)
+    derivative = shared + 0.5 * u * (1.0 - bent * bent) * (slope * (1.0 + 3.0 * 0.044715 * square))
+    return u * shared, derivative
+
+
+def block_kernel(
+    tok, cot, pre, wq_in, wf_in, wp_in, wo_in, cols_in,
+    out_hbm, grad_hbm, wq_hbm, wf_hbm, wp_hbm, wo_hbm, vec_hbm,
+    xt, gt, wqa, wfa, wpa, woa, zq, zf, zp, zo, pres, cols, colb,
+    fn, qkv, at, lse, st1, st2, mid, sn, act, slope, op, hg, sp,
+    came2, came_out, came1, br, ap, dout, brf, dqkv, ksum, vsum,
+    gf, gp, gq, near_f, near_p, near_q, sum_f, sum_p, sum_q, cross_f, cross_p, cross_q,
+    high_f, high_p, high_q, fin_f, fin_p, fin_q,
+    sq, near_o, sum_o, came_o, cross_o, high_o, fin_o,
+    fgp, vcol, vec, vec_in, stat, stat_in, out_v, grad_v,
+    send_sems, recv_sems, local_sems,
+):
+    links = Links(send_sems, recv_sems, local_sems)
+    r, c = links.r, links.c
+    mine = links.half()
+    own = aligned(r * QUARTER, QUARTER)
+    staged = [
+        links.local(tok, xt.at[r]),
+        links.local(wq_in.at[mine], zq.at[c]),
+        links.local(pre, pres.at[r]),
+        links.local(cols_in, cols),
+        links.local(wo_in.at[mine], zo.at[c]),
+        links.local(wf_in.at[mine], zf.at[c]),
+        links.local(wp_in.at[mine], zp.at[c]),
+        links.local(cot, gt.at[r]),
+    ]
+    links.meet(
+        links.partner(), *(links.plane(k) for k in (1, 2, 3)), *(links.column(k) for k in (1, 2, 3))
+    )
+    for copy in staged:
+        copy.wait()
+
+    tokens = PlaneGather(links, xt)
+    get_q = WeightGather(links, zq, wqa)
+    prefixes = [links.send(pres.at[r], pres.at[r], links.plane(k)) for k in (1, 2, 3)]
+    for j in range(7):
+        colb[j] = jnp.broadcast_to(cols[:, j : j + 1], (D, LANES))
+    tokens.relay()
+    get_q.cross()
+    get_o = SquareGather(links, zo, woa)
+    get_f = WeightGather(links, zf, wfa)
+    get_p = WeightGather(links, zp, wpa)
+    tokens.finish()
+    normalize(
+        lambda lanes: wide(merged(xt[:, :, lanes])), fn, st1, colb.at[GAIN1], colb.at[BIAS1]
+    )
+    get_q.share()
+    get_o.cross()
+    get_f.cross()
+    for copy in prefixes:
+        copy.wait()
+    get_q.finish()
+
+    def project(b):
+        lanes = aligned(b * QUARTER, QUARTER)
+        bias = colb[QKV_BIAS, :WQ]
+        value = dot(merged(wqa[...]), fn[:, lanes], 0, 0)
+        qkv[:, lanes] = low(value + jnp.concatenate([bias, bias], axis=1))
+
+    each(4, project)
+    limit_value = pres[c][0:1, 0:1]
+
+    def put_attn(rows, lanes, value):
+        at[r, rows, lanes] = value
+
+    def get_attn(rows, lanes):
+        return at[r, rows, lanes]
+
+    attend(qkv, limit_value, put_attn, lse)
+    attns = PlaneGather(links, at)
+    get_o.share()
+    get_f.share()
+    attns.relay()
+    grads = PlaneGather(links, gt)
+    get_p.cross()
+    get_o.finish()
+    attns.finish()
+
+    def join(i):
+        b, lanes = lax.div(i, 4), aligned(lax.rem(i, 4) * QUARTER, QUARTER)
+        rows = aligned(b * WIDTH, WIDTH)
+        bias = colb[OUT_BIAS, rows]
+        value = dot(merged(woa[b]), merged(at[:, :, lanes]), 0, 0)
+        mid[rows, lanes] = wide(xt[b, :, lanes]) + (value + jnp.concatenate([bias, bias], axis=1))
+
+    each(16, join)
+    normalize(lambda lanes: mid[:, lanes], sn, st2, colb.at[GAIN2], colb.at[BIAS2])
+    grads.relay()
+    get_f.finish()
+
+    def up(b):
+        lanes = aligned(b * QUARTER, QUARTER)
+        bias = colb[FC_BIAS]
+        value = dot(merged(wfa[...]), sn[:, lanes], 0, 0) + jnp.concatenate([bias, bias], axis=1)
+        value, derivative = gelu_parts(value)
+        act[:, lanes] = low(value)
+        slope[:, lanes] = derivative
+
+    each(4, up)
+    get_p.share()
+    grads.finish()
+    get_p.finish()
+
+    returns = []
+    for k in (3, 1, 2, 0):
+        lanes = aligned(links.across(k) * QUARTER, QUARTER)
+        value = dot(merged(wpa[...]), merged(gt[:, :, lanes]), 0, 0)
+        hg[:, lanes] = low(value * slope[:, lanes])
+        sp[:, lanes] = low(dot(merged(wfa[...]), hg[:, lanes], 1, 0))
+        if k:
+            returns.append(links.send(sp.at[:, lanes], came2.at[k - 1], links.plane(k)))
+
+    def weight_grads(b):
+        gp[b] = low(dot(gt[b], act[...], 1, 1))
+        gf[b] = low(dot(sn[aligned(b * WIDTH, WIDTH), :], hg[...], 1, 1))
+
+    each(4, weight_grads)
+    put_f = WeightReduce(links, gf, near_f, sum_f, cross_f, high_f, fin_f, wf_hbm)
+    put_p = WeightReduce(links, gp, near_p, sum_p, cross_p, high_p, fin_p, wp_hbm)
+
+    def down(b):
+        lanes = aligned(b * QUARTER, QUARTER)
+        value = low(dot(merged(wpa[...]), act[:, lanes], 1, 0))
+        op[:, :, lanes] = value.reshape(4, WIDTH, QUARTER)
+
+    each(4, down)
+
+    lane = lax.broadcasted_iota(jnp.int32, (D, LANES), 1)
+    total = jnp.zeros((D, 1), jnp.float32)
+    for b in range(4):
+        lanes = slice(b * QUARTER, (b + 1) * QUARTER)
+        total = total + jnp.sum(wide(hg[:, lanes]), axis=1, keepdims=True)
+    vcol[...] = jnp.where(lane == V_FC + r, total, 0.0)
+    for copy in returns:
+        copy.wait()
+
+    def back(j):
+        lanes = aligned(r * QUARTER + j * LANES, LANES)
+        part = aligned(j * LANES, LANES)
+        given = wide(sp[:, lanes]) + wide(came2[0, :, part])
+        given = given + wide(came2[1, :, part]) + wide(came2[2, :, part])
+        inverse = st2[INVERSE : INVERSE + 1, lanes]
+        unit = (mid[:, lanes] - st2[CENTER : CENTER + 1, lanes]) * inverse
+        scaled = given * colb[GAIN2]
+        plain = jnp.sum(scaled, axis=0, keepdims=True) / D
+        cross = jnp.sum(scaled * unit, axis=0, keepdims=True) / D
+        above = wide(merged(gt[:, :, lanes]))
+        branch = low(above + inverse * (scaled - plain - unit * cross))
+        br[:, :, part] = branch.reshape(4, WIDTH, LANES)
+        value = jnp.where(lane == V_GAIN2, jnp.sum(given * unit, axis=1, keepdims=True), 0.0)
+        value = jnp.where(lane == V_BIAS2, jnp.sum(given, axis=1, keepdims=True), value)
+        value = jnp.where(lane == V_OUT, jnp.sum(wide(branch), axis=1, keepdims=True), value)
+        value = jnp.where(lane == V_PROJ, jnp.sum(above, axis=1, keepdims=True), value)
+        vcol[...] = vcol[...] + value
+
+    each(2, back)
+    value = dot(merged(woa[0]), br[0], 1, 0)
+    for b in range(1, 4):
+        value = value + dot(merged(woa[b]), br[b], 1, 0)
+    ap[...] = low(value).reshape(4, WIDTH, QUARTER)
+    turns = [
+        links.send(ap.at[links.across(k)], dout.at[:, own], links.plane(k)) for k in (3, 1, 2)
+    ]
+    turns.append(links.local(ap.at[r], dout.at[:, own]))
+    swaps = [
+        links.send(br.at[links.across(k)], brf.at[:, own], links.plane(k)) for k in (3, 1, 2)
+    ]
+    swaps.append(links.local(br.at[r], brf.at[:, own]))
+
+    def square_grads(b):
+        value = low(dot(merged(at[:, :, own]), br[b], 1, 1))
+        sq[b] = value.reshape(4, WIDTH, WIDTH)
+
+    each(4, square_grads)
+    put_o = SquareReduce(links, sq, near_o, sum_o, came_o, cross_o, high_o, fin_o, wo_hbm)
+    for copy in turns:
+        copy.wait()
+    put_f.cross()
+    put_p.cross()
+    attend_back(qkv, limit_value, get_attn, lse, dout, dqkv, ksum, vsum)
+
+    stat[...] = jnp.zeros_like(stat)
+    firsts = []
+    for k in (3, 1, 2, 0):
+        b = links.across(k)
+        rows = aligned(b * WIDTH, WIDTH)
+
+        def first_part(j, b=b, rows=rows):
+            lanes = aligned(j * QUARTER, QUARTER)
+            value = dot(wqa[b], dqkv[:, lanes], 1, 0)
+            fgp[b, :, lanes] = low(value)
+            for i in range(2):
+                half = aligned(j * QUARTER + i * LANES, LANES)
+                piece = value[:, i * LANES : (i + 1) * LANES]
+                unit = wide(xt[b, :, half]) - st1[CENTER : CENTER + 1, half]
+                unit = unit * st1[INVERSE : INVERSE + 1, half]
+                weighted = piece * unit
+                gain = colb[GAIN1, rows]
+                stat[0:1, half] += jnp.sum(piece * gain, axis=0, keepdims=True)
+                stat[1:2, half] += jnp.sum(weighted * gain, axis=0, keepdims=True)
+                spot = lane[:WIDTH]
+                add = jnp.where(spot == V_GAIN1, jnp.sum(weighted, axis=1, keepdims=True), 0.0)
+                add = jnp.where(spot == V_BIAS1, jnp.sum(piece, axis=1, keepdims=True), add)
+                vcol[rows, :] = vcol[rows, :] + add
+
+        each(4, first_part)
+        if k:
+            firsts.append(links.send(fgp.at[b], came1.at[k - 1], links.plane(k)))
+    stat_sends = [links.send(stat, stat_in.at[k - 1], links.plane(k)) for k in (1, 2, 3)]
+
+    def query_grads(b):
+        gq[b] = low(dot(fn[aligned(b * WIDTH, WIDTH), :], dqkv[...], 1, 1))
+
+    each(4, query_grads)
+    put_q = WeightReduce(links, gq, near_q, sum_q, cross_q, high_q, fin_q, wq_hbm)
+    put_f.rise()
+    put_p.rise()
+    rows = aligned(r * WIDTH, WIDTH)
+    spot = lane[:WIDTH]
+    query = jnp.zeros((WIDTH, 1), jnp.float32)
+    value = jnp.zeros((WIDTH, 1), jnp.float32)
+    for b in range(4):
+        lanes = slice(b * QUARTER, (b + 1) * QUARTER)
+        query = query + jnp.sum(wide(dqkv[:WIDTH, lanes]), axis=1, keepdims=True)
+        value = value + jnp.sum(wide(dqkv[2 * WIDTH :, lanes]), axis=1, keepdims=True)
+    add = jnp.where(spot == V_QUERY, query, jnp.where(spot == V_VALUE, value, 0.0))
+    vcol[rows, :] = vcol[rows, :] + add
+    vec[0] = vcol[...].T[:16]
+    vec_near = links.send(vec.at[0], vec_in.at[0], links.partner())
+    put_o.cross()
+    put_q.cross()
+    outs = [
+        links.send(op.at[links.across(k)], came_out.at[k - 1], links.plane(k)) for k in (3, 1, 2)
+    ]
+    vec_near.wait()
+    vec[1] = vec[0] + vec_in[0]
+    vec_plane = [links.send(vec.at[1], vec_in.at[k], links.plane(k)) for k in (1, 2, 3)]
+    put_o.rise()
+    put_q.rise()
+    for copy in vec_plane:
+        copy.wait()
+    vec[2] = vec[1] + vec_in[1] + vec_in[2] + vec_in[3]
+    vec_high = [links.send(vec.at[2], vec_in.at[3 + k], links.column(k)) for k in (1, 2, 3)]
+    put_f.total()
+    put_p.total()
+    for copy in swaps + firsts + stat_sends:
+        copy.wait()
+    stat[...] = stat[...] + stat_in[0] + stat_in[1] + stat_in[2]
+
+    def last_grad(j):
+        lanes = aligned(j * LANES, LANES)
+        given = wide(fgp[r, :, lanes]) + wide(came1[0, :, lanes])
+        given = given + wide(came1[1, :, lanes]) + wide(came1[2, :, lanes])
+        inverse = st1[INVERSE : INVERSE + 1, lanes]
+        unit = (wide(xt[r, :, lanes]) - st1[CENTER : CENTER + 1, lanes]) * inverse
+        value = given * colb[GAIN1, rows] - stat[0:1, lanes] / D - unit * (stat[1:2, lanes] / D)
+        grad_v[:, lanes] = wide(brf[:, lanes]) + inverse * value
+
+    each(LEN // LANES, last_grad)
+    ends = [links.local(grad_v, grad_hbm)]
+    for copy in outs:
+        copy.wait()
+
+    def last_out(j):
+        lanes = aligned(j * LANES, LANES)
+        value = mid[rows, lanes] + cols[rows, PROJ_BIAS : PROJ_BIAS + 1] + wide(op[r, :, lanes])
+        for k in range(3):
+            value = value + wide(came_out[k, :, lanes])
+        out_v[:, lanes] = low(value)
+
+    each(LEN // LANES, last_out)
+    ends.append(links.local(out_v, out_hbm))
+    for copy in vec_high:
+        copy.wait()
+    vec[3] = vec[2] + vec_in[4] + vec_in[5] + vec_in[6]
+    ends.append(links.local(vec.at[3], vec_hbm))
+    put_o.total()
+    put_q.total()
+    for copy in ends:
+        copy.wait()
+    for put in (put_f, put_p, put_o, put_q):
+        put.finish()
+
+
+def run_block(*arguments):
+    narrow, full = jnp.bfloat16, jnp.float32
+    vmem = pltpu.VMEM
+    sequence, tall = (4, WIDTH, LEN), (D, LEN)
+
+    def reduce_buffers(kind):
+        return [vmem(kind + (HALF, width), narrow) for width in (D, D, WQ)]
+
+    scratch = [
+        vmem(sequence, narrow), vmem(sequence, narrow),
+        vmem((4, WIDTH, WQ), narrow), vmem((4, WIDTH, D), narrow), vmem((4, WIDTH, D), narrow),
+        vmem((4, 4, WIDTH, WIDTH), narrow),
+        vmem((4, HALF, WQ), narrow), vmem((4, HALF, D), narrow), vmem((4, HALF, D), narrow),
+        vmem((4, HALF, WIDTH), narrow),
+        vmem((4, 8, LANES), jnp.int32), vmem((D, 8), full), vmem((7, D, LANES), full),
+        vmem(tall, narrow), vmem((WQ, LEN), narrow), vmem(sequence, narrow),
+        vmem((8, LEN), full), vmem((8, LEN), full), vmem((8, LEN), full),
+        vmem(tall, full), vmem(tall, narrow), vmem(tall, narrow), vmem(tall, full),
+        vmem(sequence, narrow), vmem(tall, narrow), vmem(tall, narrow),
+        vmem((3, D, QUARTER), narrow), vmem((3, WIDTH, LEN), narrow), vmem((3, WIDTH, LEN), narrow),
+        vmem((4, WIDTH, QUARTER), narrow), vmem((4, WIDTH, QUARTER), narrow),
+        vmem((WIDTH, LEN), narrow), vmem((WIDTH, LEN), narrow), vmem((WQ, LEN), narrow),
+        vmem((HEAD_DIM, LEN), full), vmem((HEAD_DIM, LEN), full),
+        vmem((4, WIDTH, D), narrow), vmem((4, WIDTH, D), narrow), vmem((4, WIDTH, WQ), narrow),
+        *reduce_buffers((4,)), *reduce_buffers((4,)), *reduce_buffers((4,)), *reduce_buffers((3,)),
+        vmem((HALF, D), full), vmem((HALF, D), full), vmem((HALF, WQ), full),
+        vmem((4, 4, WIDTH, WIDTH), narrow), vmem((4, 4, HALF, WIDTH), narrow),
+        vmem((4, 4, HALF, WIDTH), narrow), vmem((3, 4, HALF, WIDTH), narrow),
+        vmem((4, HALF, WIDTH), narrow), vmem((3, HALF, WIDTH), narrow), vmem((HALF, WIDTH), full),
+        vmem(sequence, narrow), vmem((D, LANES), full),
+        vmem((4, 16, D), full), vmem((7, 16, D), full), vmem((8, LEN), full), vmem((3, 8, LEN), full),
+        vmem((WIDTH, LEN), narrow), vmem((WIDTH, LEN), full),
+        pltpu.SemaphoreType.DMA((REMOTES,)), pltpu.SemaphoreType.DMA((REMOTES,)),
+        pltpu.SemaphoreType.DMA((LOCALS,)),
+    ]
+    results = [
+        ((WIDTH, LEN), narrow), ((WIDTH, LEN), full), ((WIDTH, WQ), full), ((WIDTH, D), full),
+        ((WIDTH, D), full), ((WIDTH, WIDTH), full), ((16, D), full),
+    ]
+    return pl.pallas_call(
+        block_kernel,
+        out_shape=[jax.ShapeDtypeStruct(*result) for result in results],
+        in_specs=[ANY] * len(arguments),
+        out_specs=[ANY] * len(results),
+        scratch_shapes=scratch,
+        compiler_params=pltpu.CompilerParams(
+            collective_id=0, has_side_effects=True, vmem_limit_bytes=VMEM_LIMIT
+        ),
+        name="block",
+    )(*arguments)
+
+
+def plane_device(
+    tokens, prefix, ln1_gain, ln1_bias, w_qkv, qv_bias, w_out, out_bias,
+    ln2_gain, ln2_bias, w_fc, fc_bias, w_proj, proj_bias, cotangent,
+):
+    r = lax.axis_index("row")
+    bias = take_portion(qv_bias, r, WIDTH, 1)
+    nothing = jnp.zeros((WIDTH,), jnp.float32)
+    bias = jnp.concatenate([bias[0], nothing, bias[1], nothing])
+    columns = jnp.stack(
+        [
+            ln1_gain, ln1_bias, out_bias, ln2_gain, ln2_bias,
+            take_portion(fc_bias, r, D, 0), bias, proj_bias,
+        ],
+        axis=1,
+    )
+    output, input_grad, w_qkv_grad, w_fc_grad, w_proj_grad, w_out_grad, vector = run_block(
+        tokens,
+        cotangent,
+        jnp.broadcast_to(prefix[:, None], (8, LANES)),
+        w_qkv.transpose(1, 0, 2).reshape(WIDTH, WQ),
+        w_fc,
+        w_proj,
+        w_out,
+        columns,
+    )
+    return (
+        output,
+        input_grad,
+        vector[V_GAIN1],
+        vector[V_BIAS1],
+        w_qkv_grad.reshape(WIDTH, 3, WIDTH).transpose(1, 0, 2),
+        vector[V_QUERY : V_VALUE + 1],
+        w_out_grad,
+        vector[V_OUT],
+        vector[V_GAIN2],
+        vector[V_BIAS2],
+        w_fc_grad,
+        vector[V_FC : V_FC + 4].reshape(FF),
+        w_proj_grad,
+        vector[V_PROJ],
+    )
+
+
 def solution(mesh):
+    on_device = plane_device if dict(mesh.shape) == {"dp": 2, "row": 4, "col": 4} else general_device
     placed = (
         P("row", ("dp", "col")),
         P(("dp", "row")),

time: 1170 us -> 208 us (0.18)
  waiting for transfers between devices: 924 us -> 0 us
  Pallas kernels: 0 us -> 186 us
  matrix products: 85.4 us -> 0 us
  blocking collectives: 83.4 us -> 0 us
  other arithmetic: 37.2 us -> 0.08 us
  between operations: 15 us -> 1.36 us
    reduce_scatter x8 -> x0, waiting for transfers between devices: 597 us -> none  [the longest x4 372 us: summed_over_row(): lax.psum_scatter(term_fn(jnp.int32(0), row_count * lax.axis_size('row')),...]
    all_gather x8 -> x0, waiting for transfers between devices: 322 us -> none  [the longest x4 195 us: row_rows(): return lax.all_gather(values, 'row', axis=0, tiled=True)]
    pallas_call x0 -> x1, Pallas kernels: none -> 186 us  [run_block(): pl.pallas_call(block_kernel, out_shape=[jax.ShapeDtypeStruct(*result) for...]
    psum x5 -> x0, blocking collectives: 83.4 us -> none  [the longest x4 41.7 us: feature_totals(): return lax.psum(values, 'row')]
    dot_general x17 -> x0, matrix products: 79 us -> none  [the longest x1 7.86 us: up_term(): return jnp.dot(second_gathered, w_fc, preferred_element_type=jnp.float32)]
    reduce_sum x9 -> x0, other arithmetic: 17.4 us -> none  [the longest x1 5.65 us: on_device(): jnp.sum(hidden_grad.astype(jnp.float32), axis=0)]
    convert_element_type x8 -> x0, other arithmetic: 16.4 us -> none  [the longest x1 5.24 us: attend_backward(): score_grad = (probs * (weight_grad - row_inner)).astype(jnp.bfloat16)]
  transfers between devices with their start and end apart: 17 -> 0, of which waited for: 17 -> 0; matrix products, arithmetic and copies ran while one was open for 7% -> 0% of each run, Pallas kernels for 0% -> 0%
where the time goes in v1:
time: 208 us; the launch traced here: 207 us
  Pallas kernels  186 us (89%)
  local copies, waits for them, and re-layouts  19.8 us (10%)
    pallas_call x1, Pallas kernels, run_block(): pl.pallas_call(block_kernel, out_shape=[jax.ShapeDtypeStruct(*result) for...  186 us
    unnamed x28, local copies, waits for them, and re-layouts  9.12 us

profile of v1, /device:TPU:0, one launch (start us, length us, event | category | flops | bytes accessed | tf_op | source)
XLA Modules:
  0.0 207.3 jit_solution(14087684998606078967)
XLA Ops:
  1.3 0.6 broadcast_in_dim.12.pre
  1.9 1.1 copy.43
  3.0 0.0 copy-start.5
  3.0 0.9 copy.44.wq_in
  3.9 0.0 copy-done.5
  3.9 0.0 copy-start.6
  3.9 0.7 copy-done.6
  4.6 0.0 copy-start.7
  4.6 0.7 copy-done.7
  5.3 0.0 copy-start.8
  5.3 0.7 copy-done.8
  5.9 0.0 copy-start.9
  6.0 0.7 copy-done.9
  6.6 0.8 dynamic_slice.6
  7.4 0.8 constant_dynamic-slice_fusion
  8.3 0.1 pad_maximum_fusion
  8.3 0.0 copy-start.10
  8.3 0.7 copy-done.10
  9.1 0.9 copy.45.cols_in
  10.0 186.0 %block.1 = (bf16[192,1024]{1,0:T(8,128)(2,1)}, f32[192,1024]{1,0:T(8,128)}, f32[192,576]{1,0:T(8,128)}, f32[192,768]{1,0:T(8,128)}, f32[192,768]{1,0:T(8,128)}, /*index=5*/f32[192,192]{1,0:T(8,128)}, f32[16,768]{1,0:T(8,128)}) custom-call(bf16[192,1024]{1,0:T(8,128)(2,1)} %tok.1, bf16[192,1024]{1,0:T(8,128)(2,1)} %cot.1, s32[8,128]{1,0:T(8,128)} %broadcast_in_dim.12.pre, ...), custom_call_target="tpu_custom_call" | custom-call | tf_op jit(solution)/shard_map/block/pallas_call | solution.py:985
  196.0 1.6 slice_reduce_fusion
  197.7 1.2 copy.46
  198.9 0.0 copy-start.3
  198.9 0.0 copy-start
  198.9 1.1 copy.47
  200.0 1.3 slice.34
  201.3 0.7 slice.38
  202.1 0.6 reshape.40
  202.7 0.0 copy-done.3
  202.7 0.7 copy.54
  203.4 0.0 copy-done
  203.4 0.0 copy-start.4
  203.4 0.0 copy-start.2
  203.4 0.9 copy.55
  204.3 0.2 copy-done.4
  204.5 0.7 copy.56
  205.2 0.0 copy-done.2
  205.2 0.0 copy-start.1
  205.2 0.8 copy.57
  206.0 0.5 copy-done.1
  206.5 0.8 copy.58
  (10 shorter events, 0.1 us)
Async XLA Ops:
  3.0 0.9 copy-start.5
  3.9 0.7 copy-start.6
  4.6 0.7 copy-start.7
  5.3 0.7 copy-start.8
  5.9 0.7 copy-start.9
  8.3 0.7 copy-start.10
  198.9 3.8 %copy-start.3 = (bf16[192,1024]{1,0:T(8,128)(2,1)S(1)}, bf16[192,1024]{1,0:T(8,128)(2,1)}, u32[]{:S(2)}) copy-start(bf16[192,1024]{1,0:T(8,128)(2,1)} %get-tuple-element.78) | copy-start | bytes 1179652
  198.9 4.5 %copy-start = (f32[192,1024]{1,0:T(8,128)S(1)}, f32[192,1024]{1,0:T(8,128)}, u32[]{:S(2)}) copy-start(f32[192,1024]{1,0:T(8,128)} %get-tuple-element.79) | copy-start | bytes 2359300
  203.4 1.1 copy-start.4
  203.4 1.8 copy-start.2
  205.2 1.3 copy-start.1

commit v2 on v1

--- a/solution.py
+++ b/solution.py
@@ -311,7 +311,7 @@
 LANES = 128
 WQ = 3 * WIDTH
 VMEM_LIMIT = 67043328
-REMOTES = 112
+REMOTES = 144
 LOCALS = 40
 FACTOR = HEAD_DIM ** (-0.5)
 ANY = pl.BlockSpec(memory_space=pl.ANY)
@@ -379,6 +379,11 @@
     def half(self, mine=True):
         place = self.d if mine else 1 - self.d
         return pl.ds(pl.multiple_of(place * HALF, 16), HALF)
+
+    def crossing(self, row, place):
+        place = place + self.d * (3 - 2 * place)
+        low_bit = lax.rem(lax.rem(row, 2) + lax.rem(place, 2), 2)
+        return low_bit + 2 * lax.rem(lax.div(row, 2) + lax.div(place, 2), 2)
 
     def meet(self, *devices):
         barrier = pltpu.get_barrier_semaphore()
@@ -408,6 +413,50 @@
         return copy
 
 
+class Ticket:
+    def __init__(self, links, device):
+        self.place = links.remotes
+        links.remotes += 1
+        self.links, self.device = links, device
+
+    def __call__(self, source, target):
+        return pltpu.make_async_remote_copy(
+            src_ref=source,
+            dst_ref=target,
+            send_sem=self.links.send_sems.at[self.place],
+            recv_sem=self.links.recv_sems.at[self.place],
+            device_id=self.device,
+            device_id_type=MESH,
+        )
+
+
+class Move:
+    def __init__(self, links, stays, source, target, device):
+        self.stays = stays
+        self.ticket = Ticket(links, device)
+        self.source, self.target = source, target
+        place = links.locals
+        links.locals += 1
+        self.local_sem = links.local_sems.at[place]
+
+        @pl.when(jnp.logical_not(stays))
+        def _():
+            self.ticket(source, target).start()
+
+        @pl.when(stays)
+        def _():
+            pltpu.make_async_copy(source, target, self.local_sem).start()
+
+    def wait(self):
+        @pl.when(jnp.logical_not(self.stays))
+        def _():
+            self.ticket(self.source, self.target).wait()
+
+        @pl.when(self.stays)
+        def _():
+            pltpu.make_async_copy(self.source, self.target, self.local_sem).wait()
+
+
 class PlaneGather:
     def __init__(self, links, target):
         self.links, self.target = links, target
@@ -437,26 +486,121 @@
         self.on_x.wait()
 
 
+class PlaneReduce:
+    def __init__(self, links, part_of, rows, over_x, over_y, relayed):
+        self.links, self.part_of = links, part_of
+        self.halves = (pl.ds(0, rows // 2), pl.ds(rows // 2, rows // 2))
+        self.over_x, self.over_y, self.relayed = over_x, over_y, relayed
+        self.copies = {}
+
+    def part(self, k, half):
+        return self.part_of(self.links.across(k)).at[self.halves[half]]
+
+    def give(self, k):
+        links = self.links
+        if k == 3:
+            self.copies["x3"] = links.send(self.part(3, 0), self.over_x.at[1], links.plane(1))
+            self.copies["y3"] = links.send(self.part(3, 1), self.over_y.at[1], links.plane(2))
+        elif k == 1:
+            self.copies["x1"] = links.send(self.part(1, 0), self.over_x.at[0], links.plane(1))
+        elif k == 2:
+            self.copies["y2"] = links.send(self.part(2, 1), self.over_y.at[0], links.plane(2))
+
+    def relay(self):
+        links = self.links
+        self.copies["x3"].wait_recv()
+        add_rows(self.over_x.at[1], [self.over_x.at[1], self.part(2, 0)])
+        self.copies["xy"] = links.send(self.over_x.at[1], self.relayed.at[0], links.plane(2))
+        self.copies["y3"].wait_recv()
+        add_rows(self.over_y.at[1], [self.over_y.at[1], self.part(1, 1)])
+        self.copies["yx"] = links.send(self.over_y.at[1], self.relayed.at[1], links.plane(1))
+
+    def finish(self):
+        for name in ("x3", "y3"):
+            self.copies[name].wait_send()
+        for name in ("x1", "y2", "xy", "yx"):
+            self.copies[name].wait()
+
+    def total(self, lanes):
+        parts = []
+        for half, over in ((0, self.over_x), (1, self.over_y)):
+            value = wide(self.part(0, half)[:, lanes]) + wide(over[0, :, lanes])
+            parts.append(value + wide(self.relayed[half, :, lanes]))
+        return jnp.concatenate(parts, axis=0)
+
+
+class Line:
+    def __init__(self, links, block_of):
+        self.links, self.block_of = links, block_of
+        c = links.c
+        self.up = [Ticket(links, (links.d, links.r, lax.rem(c + 1, 4))) for _ in range(3)]
+        self.down = [Ticket(links, (links.d, links.r, lax.rem(c + 3, 4))) for _ in range(3)]
+
+    def copy(self, ticket, place):
+        return ticket(self.block_of(place), self.block_of(place))
+
+    def step(self, t):
+        c = self.links.c
+        if t > 0:
+
+            @pl.when(c >= t)
+            def _():
+                self.copy(self.up[t - 1], c - t).wait_recv()
+
+            @pl.when(c <= 3 - t)
+            def _():
+                self.copy(self.down[t - 1], c + t).wait_recv()
+
+        if t < 3:
+
+            @pl.when(jnp.logical_and(c >= t, c < 3))
+            def _():
+                self.copy(self.up[t], c - t).start()
+
+            @pl.when(jnp.logical_and(c <= 3 - t, c > 0))
+            def _():
+                self.copy(self.down[t], c + t).start()
+
+    def finish(self):
+        c = self.links.c
+        for t in range(3):
+
+            @pl.when(jnp.logical_and(c >= t, c < 3))
+            def _(t=t):
+                self.copy(self.up[t], c - t).wait_send()
+
+            @pl.when(jnp.logical_and(c <= 3 - t, c > 0))
+            def _(t=t):
+                self.copy(self.down[t], c + t).wait_send()
+
+
 class WeightGather:
-    def __init__(self, links, stage, target):
-        self.links, self.stage, self.target = links, stage, target
-        block = stage.at[links.c]
-        self.rising = [links.send(block, block, links.column(k)) for k in (2, 1, 3)]
-
-    def cross(self):
-        links, mine = self.links, self.links.half()
-        for copy in self.rising:
-            copy.wait()
-        self.crossing = [
-            links.send(self.stage.at[links.across(k)], self.target.at[links.r, mine], links.plane(k))
-            for k in (3, 1, 2)
-        ]
-        self.crossing.append(links.local(self.stage.at[links.r], self.target.at[links.r, mine]))
+    def __init__(self, links, stage, moved, target):
+        self.links, self.moved, self.target = links, moved, target
+        r, c = links.r, links.c
+        self.mine = links.half()
+        self.goal = links.crossing(r, c)
+        self.turn = Move(links, self.goal == c, stage, moved, (links.d, r, self.goal))
+
+    def hop(self):
+        links = self.links
+        self.turn.wait()
+        block = self.target.at[links.r, self.mine]
+        device = (links.d, self.goal, links.c)
+        self.turn = Move(links, self.goal == links.r, self.moved, block, device)
+
+    def block_of(self, place):
+        return self.target.at[self.links.crossing(self.links.r, place), self.mine]
+
+    def line(self, t):
+        if t == 0:
+            self.turn.wait()
+            self.way = Line(self.links, self.block_of)
+        self.way.step(t)
 
     def share(self):
-        for copy in self.crossing:
-            copy.wait()
-        block = self.target.at[:, self.links.half()]
+        self.way.finish()
+        block = self.target.at[:, self.mine]
         self.shared = self.links.send(block, block, self.links.partner())
 
     def finish(self):
@@ -464,18 +608,23 @@
 
 
 class SquareGather(WeightGather):
-    def cross(self):
-        links, mine = self.links, self.links.half()
-        for copy in self.rising:
-            copy.wait()
-        block = self.target.at[links.r, :, mine]
-        self.crossing = [links.send(self.stage, block, links.plane(k)) for k in (3, 1, 2)]
-        self.crossing.append(links.local(self.stage, block))
+    def __init__(self, links, target):
+        self.links, self.target = links, target
+        self.mine = links.half()
+        self.plane = PlaneGather(links, target.at[:, links.c, self.mine])
+
+    def block_of(self, place):
+        return self.target.at[:, place, self.mine]
+
+    def line(self, t):
+        if t == 0:
+            self.plane.finish()
+            self.way = Line(self.links, self.block_of)
+        self.way.step(t)
 
     def share(self):
-        for copy in self.crossing:
-            copy.wait()
-        block = self.target.at[:, :, self.links.half()]
+        self.way.finish()
+        block = self.target.at[:, :, self.mine]
         self.shared = self.links.send(block, block, self.links.partner())
 
 
@@ -490,41 +639,110 @@
     each(target.shape[0] // 16, step)
 
 
+def add_blocks(target, terms):
+    if len(target.shape) == 2:
+        add_rows(target, terms)
+    else:
+        each(target.shape[0], lambda i: add_blocks(target.at[i], [term.at[i] for term in terms]))
+
+
+class LineReduce:
+    def __init__(self, links, block_of, up, down):
+        self.links, self.block_of, self.up, self.down = links, block_of, up, down
+        c = links.c
+        self.rise = [Ticket(links, (links.d, links.r, lax.rem(c + 1, 4))) for _ in range(3)]
+        self.fall = [Ticket(links, (links.d, links.r, lax.rem(c + 3, 4))) for _ in range(3)]
+
+    def step(self, i):
+        c = self.links.c
+        goal = 3 - i
+        slot = self.up.at[goal - 1]
+        self.pass_on(self.rise[goal - 1], slot, goal, c == 0, jnp.logical_and(c > 0, c < goal))
+        goal = i
+        slot = self.down.at[goal]
+        self.pass_on(self.fall[goal], slot, goal, c == 3, jnp.logical_and(c < 3, c > goal))
+
+    def pass_on(self, ticket, slot, goal, begins, adds):
+        @pl.when(begins)
+        def _():
+            ticket(self.block_of(goal), slot).start()
+
+        @pl.when(adds)
+        def _():
+            ticket(slot, slot).wait_recv()
+            add_blocks(slot, [slot, self.block_of(goal)])
+            ticket(slot, slot).start()
+
+    def total(self, target):
+        c = self.links.c
+        for goal in range(4):
+
+            @pl.when(c == goal)
+            def _(goal=goal):
+                terms = [self.block_of(goal)]
+                if goal > 0:
+                    slot = self.up.at[goal - 1]
+                    self.rise[goal - 1](slot, slot).wait_recv()
+                    terms.append(slot)
+                if goal < 3:
+                    slot = self.down.at[goal]
+                    self.fall[goal](slot, slot).wait_recv()
+                    terms.append(slot)
+                add_blocks(target, terms)
+
+        for i in range(3):
+            rising, falling = self.up.at[i], self.down.at[i]
+
+            @pl.when(c < i + 1)
+            def _(i=i, slot=rising):
+                self.rise[i](slot, slot).wait_send()
+
+            @pl.when(c > i)
+            def _(i=i, slot=falling):
+                self.fall[i](slot, slot).wait_send()
+
+
 class WeightReduce:
-    def __init__(self, links, grad, near, sums, cross, high, final, result):
+    def __init__(self, links, grad, near, sums, up, down, fin, moved, arrived, result):
         self.links, self.grad, self.near, self.sums = links, grad, near, sums
-        self.crossed, self.high, self.final, self.result = cross, high, final, result
+        self.up, self.down, self.fin = up, down, fin
+        self.moved, self.arrived, self.result = moved, arrived, result
         self.to_near = links.send(grad.at[:, links.half(False)], near, links.partner())
 
-    def cross(self):
+    def block_of(self, place):
+        return self.sums.at[self.links.crossing(self.links.r, place)]
+
+    def add_near(self):
+        mine = self.links.half()
+        self.to_near.wait()
+        each(4, lambda b: add_rows(self.sums.at[b], [self.grad.at[b, mine], self.near.at[b]]))
+        self.way = LineReduce(self.links, self.block_of, self.up, self.down)
+
+    def line(self, i):
+        self.way.step(i)
+
+    def hop(self):
+        links = self.links
+        self.way.total(self.fin)
+        self.goal = links.crossing(links.r, links.c)
+        device = (links.d, self.goal, links.c)
+        self.turn = Move(links, self.goal == links.r, self.fin, self.moved, device)
+
+    def back(self):
+        links = self.links
+        self.turn.wait()
+        device = (links.d, links.r, self.goal)
+        self.turn = Move(links, self.goal == links.c, self.moved, self.arrived, device)
+
+    def share(self):
+        self.turn.wait()
+        self.give(self.arrived)
+
+    def give(self, total):
         links, mine = self.links, self.links.half()
-        self.to_near.wait()
-        for b in range(4):
-            add_rows(self.sums.at[b], [self.grad.at[b, mine], self.near.at[b]])
-        self.crossing = [
-            links.send(self.sums.at[links.across(k)], self.crossed.at[links.r], links.plane(k))
-            for k in (3, 1, 2)
-        ]
-        self.crossing.append(links.local(self.sums.at[links.r], self.crossed.at[links.r]))
-
-    def rise(self):
-        links = self.links
-        for copy in self.crossing:
-            copy.wait()
-        self.rising = [
-            links.send(self.crossed.at[links.height(k)], self.high.at[k - 1], links.column(k))
-            for k in (2, 1, 3)
-        ]
-
-    def total(self):
-        links, mine = self.links, self.links.half()
-        for copy in self.rising:
-            copy.wait()
-        high = self.high
-        add_rows(self.final, [self.crossed.at[links.c], high.at[0], high.at[1], high.at[2]])
         self.last = [
-            links.send(self.final, self.result.at[mine], links.partner()),
-            links.local(self.final, self.result.at[mine]),
+            links.send(total, self.result.at[mine], links.partner()),
+            links.local(total, self.result.at[mine]),
         ]
 
     def finish(self):
@@ -533,37 +751,37 @@
 
 
 class SquareReduce(WeightReduce):
-    def __init__(self, links, grad, near, sums, came, cross, high, final, result):
-        self.came = came
+    def __init__(self, links, grad, near, sums, up, down, fin, came, arrived, result):
         self.links, self.grad, self.near, self.sums = links, grad, near, sums
-        self.crossed, self.high, self.final, self.result = cross, high, final, result
+        self.up, self.down, self.fin = up, down, fin
+        self.came, self.arrived, self.result = came, arrived, result
         self.to_near = links.send(grad.at[:, :, links.half(False)], near, links.partner())
 
-    def cross(self):
-        links, mine = self.links, self.links.half()
+    def block_of(self, place):
+        return self.sums.at[:, place]
+
+    def add_near(self):
+        mine = self.links.half()
         self.to_near.wait()
-
-        def add(i):
-            b, e = lax.div(i, 4), lax.rem(i, 4)
-            add_rows(self.sums.at[b, e], [self.grad.at[b, e, mine], self.near.at[b, e]])
-
-        each(16, add)
+        add_blocks(self.sums, [self.grad.at[:, :, mine], self.near])
+        self.way = LineReduce(self.links, self.block_of, self.up, self.down)
+
+    def hop(self):
+        links = self.links
+        self.way.total(self.fin)
         self.crossing = [
-            links.send(self.sums.at[links.across(k)], self.came.at[k - 1], links.plane(k))
+            links.send(self.fin.at[links.across(k)], self.came.at[k - 1], links.plane(k))
             for k in (3, 1, 2)
         ]
 
-    def rise(self):
+    def back(self):
         for copy in self.crossing:
             copy.wait()
-
-        def add(e):
-            terms = [self.sums.at[self.links.r, e]] + [self.came.at[k, e] for k in range(3)]
-            add_rows(self.crossed.at[e], terms)
-
-        each(4, add)
-        self.crossing = []
-        WeightReduce.rise(self)
+        came = self.came
+        add_rows(self.arrived, [self.fin.at[self.links.r], came.at[0], came.at[1], came.at[2]])
+
+    def share(self):
+        self.give(self.arrived)
 
 
 def normalize(source_of, target, stats, gain, offset):
@@ -598,11 +816,12 @@
 
 
 def head_rows(h, part):
-    return pl.ds(pl.multiple_of(h * HEAD_DIM + part * WIDTH, HEAD_DIM), HEAD_DIM)
-
-
-def attend(qkv, limit_value, attn_of, log_total):
+    return pl.ds(h * HEAD_DIM + part * WIDTH, HEAD_DIM)
+
+
+def attend(qkv, limit_value, attn_of, log_total, between):
     def head(h):
+        between[h]()
         for block in range(4):
             last, _ = key_span(block)
             lanes = slice(block * QUARTER, (block + 1) * QUARTER)
@@ -616,11 +835,15 @@
             attn_of(head_rows(h, 0), lanes, low(mixed * (1.0 / total)))
             log_total[pl.ds(h, 1), lanes] = largest + jnp.log(total)
 
-    each(3, head)
-
-
-def attend_back(qkv, limit_value, attn_of, log_total, out_grad, qkv_grad, key_sum, value_sum):
+    for h in range(3):
+        head(h)
+
+
+def attend_back(
+    qkv, limit_value, attn_of, log_total, out_grad, qkv_grad, key_sum, value_sum, between
+):
     def head(h):
+        between[h]()
         for block in (3, 2, 1, 0):
             last, _ = key_span(block)
             lanes = slice(block * QUARTER, (block + 1) * QUARTER)
@@ -647,7 +870,8 @@
         qkv_grad[head_rows(h, 1), :] = low(key_sum[...])
         qkv_grad[head_rows(h, 2), :] = low(value_sum[...])
 
-    each(3, head)
+    for h in range(3):
+        head(h)
 
 
 def gelu_parts(u):
@@ -659,15 +883,23 @@
     return u * shared, derivative
 
 
+def in_turn(*actions):
+    def run():
+        for action in actions:
+            action()
+
+    return run
+
+
 def block_kernel(
     tok, cot, pre, wq_in, wf_in, wp_in, wo_in, cols_in,
     out_hbm, grad_hbm, wq_hbm, wf_hbm, wp_hbm, wo_hbm, vec_hbm,
-    xt, gt, wqa, wfa, wpa, woa, zq, zf, zp, zo, pres, cols, colb,
+    xt, gt, wqa, wfa, wpa, woa, zq, zf, zp, mq, mf, mp, pres, cols, colb,
     fn, qkv, at, lse, st1, st2, mid, sn, act, slope, op, hg, sp,
-    came2, came_out, came1, br, ap, dout, brf, dqkv, ksum, vsum,
-    gf, gp, gq, near_f, near_p, near_q, sum_f, sum_p, sum_q, cross_f, cross_p, cross_q,
-    high_f, high_p, high_q, fin_f, fin_p, fin_q,
-    sq, near_o, sum_o, came_o, cross_o, high_o, fin_o,
+    x2, y2, z2, x_out, y_out, z_out, x1, y1, z1, br, ap, dout, brf, dqkv, ksum, vsum,
+    gf, gp, gq, near_f, near_p, near_q, sum_f, sum_p, sum_q, up_f, up_p, up_q, dn_f, dn_p, dn_q,
+    fin_f, fin_p, fin_q, hop_f, hop_p, hop_q, got_f, got_p, got_q,
+    sq, near_o, sum_o, up_o, dn_o, fin_o, hop_o, got_o,
     fgp, vcol, vec, vec_in, stat, stat_in, out_v, grad_v,
     send_sems, recv_sems, local_sems,
 ):
@@ -677,12 +909,12 @@
     own = aligned(r * QUARTER, QUARTER)
     staged = [
         links.local(tok, xt.at[r]),
-        links.local(wq_in.at[mine], zq.at[c]),
+        links.local(wq_in.at[mine], zq),
         links.local(pre, pres.at[r]),
         links.local(cols_in, cols),
-        links.local(wo_in.at[mine], zo.at[c]),
-        links.local(wf_in.at[mine], zf.at[c]),
-        links.local(wp_in.at[mine], zp.at[c]),
+        links.local(wo_in.at[mine], woa.at[r, c, mine]),
+        links.local(wf_in.at[mine], zf),
+        links.local(wp_in.at[mine], zp),
         links.local(cot, gt.at[r]),
     ]
     links.meet(
@@ -691,25 +923,30 @@
     for copy in staged:
         copy.wait()
 
+    get_q = WeightGather(links, zq, mq, wqa)
     tokens = PlaneGather(links, xt)
-    get_q = WeightGather(links, zq, wqa)
     prefixes = [links.send(pres.at[r], pres.at[r], links.plane(k)) for k in (1, 2, 3)]
+    get_o = SquareGather(links, woa)
     for j in range(7):
         colb[j] = jnp.broadcast_to(cols[:, j : j + 1], (D, LANES))
+    get_q.hop()
+    get_o.plane.relay()
+    get_q.line(0)
     tokens.relay()
-    get_q.cross()
-    get_o = SquareGather(links, zo, woa)
-    get_f = WeightGather(links, zf, wfa)
-    get_p = WeightGather(links, zp, wpa)
+    get_q.line(1)
+    get_q.line(2)
+    get_o.line(0)
+    get_q.line(3)
+    get_q.share()
     tokens.finish()
+    grads = PlaneGather(links, gt)
     normalize(
         lambda lanes: wide(merged(xt[:, :, lanes])), fn, st1, colb.at[GAIN1], colb.at[BIAS1]
     )
-    get_q.share()
-    get_o.cross()
-    get_f.cross()
     for copy in prefixes:
         copy.wait()
+    get_o.line(1)
+    get_f = WeightGather(links, zf, mf, wfa)
     get_q.finish()
 
     def project(b):
@@ -727,14 +964,29 @@
     def get_attn(rows, lanes):
         return at[r, rows, lanes]
 
-    attend(qkv, limit_value, put_attn, lse)
+    attend(
+        qkv,
+        limit_value,
+        put_attn,
+        lse,
+        [
+            in_turn(lambda: get_o.line(2), get_f.hop),
+            in_turn(lambda: get_o.line(3), lambda: get_f.line(0), grads.relay),
+            lambda: get_f.line(1),
+        ],
+    )
     attns = PlaneGather(links, at)
+    get_p = WeightGather(links, zp, mp, wpa)
     get_o.share()
+    get_f.line(2)
+    get_p.hop()
+    get_f.line(3)
     get_f.share()
+    get_p.line(0)
     attns.relay()
-    grads = PlaneGather(links, gt)
-    get_p.cross()
     get_o.finish()
+    grads.finish()
+    get_p.line(1)
     attns.finish()
 
     def join(i):
@@ -745,8 +997,10 @@
         mid[rows, lanes] = wide(xt[b, :, lanes]) + (value + jnp.concatenate([bias, bias], axis=1))
 
     each(16, join)
+    get_p.line(2)
     normalize(lambda lanes: mid[:, lanes], sn, st2, colb.at[GAIN2], colb.at[BIAS2])
-    grads.relay()
+    get_p.line(3)
+    get_p.share()
     get_f.finish()
 
     def up(b):
@@ -758,26 +1012,31 @@
         slope[:, lanes] = derivative
 
     each(4, up)
-    get_p.share()
-    grads.finish()
     get_p.finish()
 
-    returns = []
+    seconds = PlaneReduce(
+        links, lambda place: sp.at[:, aligned(place * QUARTER, QUARTER)], D, x2, y2, z2
+    )
     for k in (3, 1, 2, 0):
         lanes = aligned(links.across(k) * QUARTER, QUARTER)
         value = dot(merged(wpa[...]), merged(gt[:, :, lanes]), 0, 0)
         hg[:, lanes] = low(value * slope[:, lanes])
         sp[:, lanes] = low(dot(merged(wfa[...]), hg[:, lanes], 1, 0))
-        if k:
-            returns.append(links.send(sp.at[:, lanes], came2.at[k - 1], links.plane(k)))
-
-    def weight_grads(b):
+        seconds.give(k)
+
+    def proj_grads(b):
         gp[b] = low(dot(gt[b], act[...], 1, 1))
+
+    def fc_grads(b):
         gf[b] = low(dot(sn[aligned(b * WIDTH, WIDTH), :], hg[...], 1, 1))
 
-    each(4, weight_grads)
-    put_f = WeightReduce(links, gf, near_f, sum_f, cross_f, high_f, fin_f, wf_hbm)
-    put_p = WeightReduce(links, gp, near_p, sum_p, cross_p, high_p, fin_p, wp_hbm)
+    each(4, proj_grads)
+    put_p = WeightReduce(links, gp, near_p, sum_p, up_p, dn_p, fin_p, hop_p, got_p, wp_hbm)
+    seconds.relay()
+    each(4, fc_grads)
+    put_f = WeightReduce(links, gf, near_f, sum_f, up_f, dn_f, fin_f, hop_f, got_f, wf_hbm)
+    put_p.add_near()
+    put_p.line(0)
 
     def down(b):
         lanes = aligned(b * QUARTER, QUARTER)
@@ -785,6 +1044,7 @@
         op[:, :, lanes] = value.reshape(4, WIDTH, QUARTER)
 
     each(4, down)
+    outs = PlaneReduce(links, lambda place: op.at[place], WIDTH, x_out, y_out, z_out)
 
     lane = lax.broadcasted_iota(jnp.int32, (D, LANES), 1)
     total = jnp.zeros((D, 1), jnp.float32)
@@ -792,14 +1052,16 @@
         lanes = slice(b * QUARTER, (b + 1) * QUARTER)
         total = total + jnp.sum(wide(hg[:, lanes]), axis=1, keepdims=True)
     vcol[...] = jnp.where(lane == V_FC + r, total, 0.0)
-    for copy in returns:
-        copy.wait()
+    put_p.line(1)
+    put_f.add_near()
+    put_p.line(2)
+    put_f.line(0)
+    seconds.finish()
 
     def back(j):
         lanes = aligned(r * QUARTER + j * LANES, LANES)
         part = aligned(j * LANES, LANES)
-        given = wide(sp[:, lanes]) + wide(came2[0, :, part])
-        given = given + wide(came2[1, :, part]) + wide(came2[2, :, part])
+        given = seconds.total(part)
         inverse = st2[INVERSE : INVERSE + 1, lanes]
         unit = (mid[:, lanes] - st2[CENTER : CENTER + 1, lanes]) * inverse
         scaled = given * colb[GAIN2]
@@ -814,7 +1076,8 @@
         value = jnp.where(lane == V_PROJ, jnp.sum(above, axis=1, keepdims=True), value)
         vcol[...] = vcol[...] + value
 
-    each(2, back)
+    for j in range(2):
+        back(j)
     value = dot(merged(woa[0]), br[0], 1, 0)
     for b in range(1, 4):
         value = value + dot(merged(woa[b]), br[b], 1, 0)
@@ -833,15 +1096,32 @@
         sq[b] = value.reshape(4, WIDTH, WIDTH)
 
     each(4, square_grads)
-    put_o = SquareReduce(links, sq, near_o, sum_o, came_o, cross_o, high_o, fin_o, wo_hbm)
+    put_o = SquareReduce(links, sq, near_o, sum_o, up_o, dn_o, fin_o, hop_o, got_o, wo_hbm)
+    put_p.hop()
+    put_f.line(1)
+    put_f.line(2)
+    put_o.add_near()
     for copy in turns:
         copy.wait()
-    put_f.cross()
-    put_p.cross()
-    attend_back(qkv, limit_value, get_attn, lse, dout, dqkv, ksum, vsum)
+    for k in (3, 1, 2):
+        outs.give(k)
+    attend_back(
+        qkv, limit_value, get_attn, lse, dout, dqkv, ksum, vsum,
+        [
+            in_turn(put_p.back, lambda: put_o.line(0)),
+            in_turn(put_f.hop, lambda: put_o.line(1)),
+            in_turn(outs.relay, put_p.share, lambda: put_o.line(2)),
+        ],
+    )
+
+    def query_grads(b):
+        gq[b] = low(dot(fn[aligned(b * WIDTH, WIDTH), :], dqkv[...], 1, 1))
+
+    each(4, query_grads)
+    put_q = WeightReduce(links, gq, near_q, sum_q, up_q, dn_q, fin_q, hop_q, got_q, wq_hbm)
 
     stat[...] = jnp.zeros_like(stat)
-    firsts = []
+    firsts = PlaneReduce(links, lambda place: fgp.at[place], WIDTH, x1, y1, z1)
     for k in (3, 1, 2, 0):
         b = links.across(k)
         rows = aligned(b * WIDTH, WIDTH)
@@ -865,17 +1145,17 @@
                 vcol[rows, :] = vcol[rows, :] + add
 
         each(4, first_part)
-        if k:
-            firsts.append(links.send(fgp.at[b], came1.at[k - 1], links.plane(k)))
+        firsts.give(k)
+        if k == 3:
+            put_q.add_near()
+            put_q.line(0)
+        elif k == 2:
+            put_q.line(1)
     stat_sends = [links.send(stat, stat_in.at[k - 1], links.plane(k)) for k in (1, 2, 3)]
-
-    def query_grads(b):
-        gq[b] = low(dot(fn[aligned(b * WIDTH, WIDTH), :], dqkv[...], 1, 1))
-
-    each(4, query_grads)
-    put_q = WeightReduce(links, gq, near_q, sum_q, cross_q, high_q, fin_q, wq_hbm)
-    put_f.rise()
-    put_p.rise()
+    put_q.line(2)
+    firsts.relay()
+    put_f.back()
+    put_o.hop()
     rows = aligned(r * WIDTH, WIDTH)
     spot = lane[:WIDTH]
     query = jnp.zeros((WIDTH, 1), jnp.float32)
@@ -888,55 +1168,46 @@
     vcol[rows, :] = vcol[rows, :] + add
     vec[0] = vcol[...].T[:16]
     vec_near = links.send(vec.at[0], vec_in.at[0], links.partner())
-    put_o.cross()
-    put_q.cross()
-    outs = [
-        links.send(op.at[links.across(k)], came_out.at[k - 1], links.plane(k)) for k in (3, 1, 2)
-    ]
+    put_q.hop()
     vec_near.wait()
     vec[1] = vec[0] + vec_in[0]
     vec_plane = [links.send(vec.at[1], vec_in.at[k], links.plane(k)) for k in (1, 2, 3)]
-    put_o.rise()
-    put_q.rise()
+    put_f.share()
+    put_o.back()
+    put_q.back()
+    put_o.share()
     for copy in vec_plane:
         copy.wait()
     vec[2] = vec[1] + vec_in[1] + vec_in[2] + vec_in[3]
     vec_high = [links.send(vec.at[2], vec_in.at[3 + k], links.column(k)) for k in (1, 2, 3)]
-    put_f.total()
-    put_p.total()
-    for copy in swaps + firsts + stat_sends:
+    outs.finish()
+
+    def last_out(j):
+        lanes = aligned(j * LANES, LANES)
+        value = mid[rows, lanes] + cols[rows, PROJ_BIAS : PROJ_BIAS + 1] + outs.total(lanes)
+        out_v[:, lanes] = low(value)
+
+    each(LEN // LANES, last_out)
+    ends = [links.local(out_v, out_hbm)]
+    for copy in swaps + stat_sends:
         copy.wait()
+    firsts.finish()
     stat[...] = stat[...] + stat_in[0] + stat_in[1] + stat_in[2]
 
     def last_grad(j):
         lanes = aligned(j * LANES, LANES)
-        given = wide(fgp[r, :, lanes]) + wide(came1[0, :, lanes])
-        given = given + wide(came1[1, :, lanes]) + wide(came1[2, :, lanes])
         inverse = st1[INVERSE : INVERSE + 1, lanes]
         unit = (wide(xt[r, :, lanes]) - st1[CENTER : CENTER + 1, lanes]) * inverse
-        value = given * colb[GAIN1, rows] - stat[0:1, lanes] / D - unit * (stat[1:2, lanes] / D)
-        grad_v[:, lanes] = wide(brf[:, lanes]) + inverse * value
+        value = firsts.total(lanes) * colb[GAIN1, rows] - stat[0:1, lanes] / D
+        grad_v[:, lanes] = wide(brf[:, lanes]) + inverse * (value - unit * (stat[1:2, lanes] / D))
 
     each(LEN // LANES, last_grad)
-    ends = [links.local(grad_v, grad_hbm)]
-    for copy in outs:
-        copy.wait()
-
-    def last_out(j):
-        lanes = aligned(j * LANES, LANES)
-        value = mid[rows, lanes] + cols[rows, PROJ_BIAS : PROJ_BIAS + 1] + wide(op[r, :, lanes])
-        for k in range(3):
-            value = value + wide(came_out[k, :, lanes])
-        out_v[:, lanes] = low(value)
-
-    each(LEN // LANES, last_out)
-    ends.append(links.local(out_v, out_hbm))
+    ends.append(links.local(grad_v, grad_hbm))
+    put_q.share()
     for copy in vec_high:
         copy.wait()
     vec[3] = vec[2] + vec_in[4] + vec_in[5] + vec_in[6]
     ends.append(links.local(vec.at[3], vec_hbm))
-    put_o.total()
-    put_q.total()
     for copy in ends:
         copy.wait()
     for put in (put_f, put_p, put_o, put_q):
@@ -948,30 +1219,33 @@
     vmem = pltpu.VMEM
     sequence, tall = (4, WIDTH, LEN), (D, LEN)
 
-    def reduce_buffers(kind):
-        return [vmem(kind + (HALF, width), narrow) for width in (D, D, WQ)]
+    def thirds(lead=()):
+        return [vmem(lead + (HALF, width), narrow) for width in (D, D, WQ)]
+
+    def plane_sums(rows, lanes):
+        return [vmem((2, rows // 2, lanes), narrow) for _ in range(3)]
 
     scratch = [
         vmem(sequence, narrow), vmem(sequence, narrow),
         vmem((4, WIDTH, WQ), narrow), vmem((4, WIDTH, D), narrow), vmem((4, WIDTH, D), narrow),
         vmem((4, 4, WIDTH, WIDTH), narrow),
-        vmem((4, HALF, WQ), narrow), vmem((4, HALF, D), narrow), vmem((4, HALF, D), narrow),
-        vmem((4, HALF, WIDTH), narrow),
+        vmem((HALF, WQ), narrow), vmem((HALF, D), narrow), vmem((HALF, D), narrow),
+        vmem((HALF, WQ), narrow), vmem((HALF, D), narrow), vmem((HALF, D), narrow),
         vmem((4, 8, LANES), jnp.int32), vmem((D, 8), full), vmem((7, D, LANES), full),
         vmem(tall, narrow), vmem((WQ, LEN), narrow), vmem(sequence, narrow),
         vmem((8, LEN), full), vmem((8, LEN), full), vmem((8, LEN), full),
         vmem(tall, full), vmem(tall, narrow), vmem(tall, narrow), vmem(tall, full),
         vmem(sequence, narrow), vmem(tall, narrow), vmem(tall, narrow),
-        vmem((3, D, QUARTER), narrow), vmem((3, WIDTH, LEN), narrow), vmem((3, WIDTH, LEN), narrow),
+        *plane_sums(D, QUARTER), *plane_sums(WIDTH, LEN), *plane_sums(WIDTH, LEN),
         vmem((4, WIDTH, QUARTER), narrow), vmem((4, WIDTH, QUARTER), narrow),
         vmem((WIDTH, LEN), narrow), vmem((WIDTH, LEN), narrow), vmem((WQ, LEN), narrow),
         vmem((HEAD_DIM, LEN), full), vmem((HEAD_DIM, LEN), full),
         vmem((4, WIDTH, D), narrow), vmem((4, WIDTH, D), narrow), vmem((4, WIDTH, WQ), narrow),
-        *reduce_buffers((4,)), *reduce_buffers((4,)), *reduce_buffers((4,)), *reduce_buffers((3,)),
-        vmem((HALF, D), full), vmem((HALF, D), full), vmem((HALF, WQ), full),
+        *thirds((4,)), *thirds((4,)), *thirds((3,)), *thirds((3,)), *thirds(), *thirds(), *thirds(),
         vmem((4, 4, WIDTH, WIDTH), narrow), vmem((4, 4, HALF, WIDTH), narrow),
         vmem((4, 4, HALF, WIDTH), narrow), vmem((3, 4, HALF, WIDTH), narrow),
-        vmem((4, HALF, WIDTH), narrow), vmem((3, HALF, WIDTH), narrow), vmem((HALF, WIDTH), full),
+        vmem((3, 4, HALF, WIDTH), narrow), vmem((4, HALF, WIDTH), narrow),
+        vmem((3, HALF, WIDTH), narrow), vmem((HALF, WIDTH), narrow),
         vmem(sequence, narrow), vmem((D, LANES), full),
         vmem((4, 16, D), full), vmem((7, 16, D), full), vmem((8, LEN), full), vmem((3, 8, LEN), full),
         vmem((WIDTH, LEN), narrow), vmem((WIDTH, LEN), full),
@@ -979,8 +1253,8 @@
         pltpu.SemaphoreType.DMA((LOCALS,)),
     ]
     results = [
-        ((WIDTH, LEN), narrow), ((WIDTH, LEN), full), ((WIDTH, WQ), full), ((WIDTH, D), full),
-        ((WIDTH, D), full), ((WIDTH, WIDTH), full), ((16, D), full),
+        ((WIDTH, LEN), narrow), ((WIDTH, LEN), full), ((WIDTH, WQ), narrow), ((WIDTH, D), narrow),
+        ((WIDTH, D), narrow), ((WIDTH, WIDTH), narrow), ((16, D), full),
     ]
     return pl.pallas_call(
         block_kernel,
@@ -1025,15 +1299,15 @@
         input_grad,
         vector[V_GAIN1],
         vector[V_BIAS1],
-        w_qkv_grad.reshape(WIDTH, 3, WIDTH).transpose(1, 0, 2),
+        wide(w_qkv_grad.reshape(WIDTH, 3, WIDTH).transpose(1, 0, 2)),
         vector[V_QUERY : V_VALUE + 1],
-        w_out_grad,
+        wide(w_out_grad),
         vector[V_OUT],
         vector[V_GAIN2],
         vector[V_BIAS2],
-        w_fc_grad,
+        wide(w_fc_grad),
         vector[V_FC : V_FC + 4].reshape(FF),
-        w_proj_grad,
+        wide(w_proj_grad),
         vector[V_PROJ],
     )
 

time: 208 us -> 215 us (1.034)
  Pallas kernels: 186 us -> 194 us
  local copies, waits for them, and re-layouts: 19.8 us -> 16.8 us
  other arithmetic: 0.08 us -> 2.48 us
    pallas_call x1, Pallas kernels: 186 us -> 194 us  [run_block(): pl.pallas_call(block_kernel, out_shape=[jax.ShapeDtypeStruct(*result) for...]
    unnamed x28 -> x15, local copies, waits for them, and re-layouts: 9.12 us -> 2.89 us
    another operation x10, local copies, waits for them, and re-layouts: 0.99 us -> 5.11 us  [plane_device(): jnp.stack([ln1_gain, ln1_bias, out_bias, ln2_gain, ln2_bias, take_portion...]
    convert_element_type x0 -> x3, other arithmetic: none -> 2.4 us  [wide(): return value.astype(jnp.float32)]
where the time goes in v2:
time: 215 us; the launch traced here: 214 us
  Pallas kernels  194 us (90%)
  local copies, waits for them, and re-layouts  16.8 us (8%)
  other arithmetic  2.48 us (1%)
    pallas_call x1, Pallas kernels, run_block(): pl.pallas_call(block_kernel, out_shape=[jax.ShapeDtypeStruct(*result) for...  194 us
    another operation x10, local copies, waits for them, and re-layouts, plane_device(): jnp.stack([ln1_gain, ln1_bias, out_bias, ln2_gain, ln2_bias, take_portion...  5.11 us

profile of v2, /device:TPU:0, one launch (start us, length us, event | category | flops | bytes accessed | tf_op | source)
XLA Modules:
  0.0 214.2 jit_solution(2959030805624662779)
XLA Ops:
  0.6 0.0 copy-start.4
  0.7 0.8 constant_dynamic-slice_fusion
  1.5 0.1 pad_maximum_fusion
  1.6 0.8 dynamic_slice.6
  2.4 0.7 stack.27
  3.1 0.7 stack.28
  3.7 0.7 stack.29
  4.4 0.7 stack.30
  5.1 0.7 stack.31
  5.8 0.7 stack.34
  6.6 0.9 copy.45.cols_in
  7.5 0.0 copy-done.4
  7.5 0.2 copy.43
  7.6 0.9 copy.44.wq_in
  9.1 0.6 broadcast_in_dim.12.pre
  9.7 193.6 %block.1 = (bf16[192,1024]{1,0:T(8,128)(2,1)}, f32[192,1024]{1,0:T(8,128)}, bf16[192,576]{1,0:T(8,128)(2,1)}, bf16[192,768]{1,0:T(8,128)(2,1)}, bf16[192,768]{1,...) custom-call(bf16[192,1024]{1,0:T(8,128)(2,1)} %tok.1, bf16[192,1024]{1,0:T(8,128)(2,1)} %cot.1, ...), custom_call_target="tpu_custom_call" | custom-call | tf_op jit(solution)/shard_map/block/pallas_call | solution.py:1259
  203.3 1.8 slice_reduce_fusion
  205.1 0.7 slice.38
  205.8 0.6 reshape.39
  206.4 1.3 slice.34
  207.8 1.1 copy.46
  208.9 0.0 copy-start.3
  208.9 1.1 copy.47
  209.9 0.0 copy-done.3
  209.9 0.0 copy-start.2
  210.0 0.0 copy-start.5
  210.0 0.9 convert_element_type.22
  210.8 0.2 copy-done.2
  211.0 0.0 copy-start.1
  211.0 0.0 copy-start
  211.0 0.9 convert_element_type.23
  211.8 0.0 copy-done.5
  211.8 0.7 convert_element_type.21
  212.5 0.0 copy-done.1
  212.5 0.7 copy.51
  213.3 0.0 copy-done
  213.3 0.9 copy.52
  (4 shorter events, 0.1 us)
Async XLA Ops:
  0.6 6.8 %copy-start.4 = (bf16[3,192,192]{2,1,0:T(8,128)(2,1)S(1)}, bf16[3,192,192]{2,1,0:T(8,128)(2,1)}, u32[]{:S(2)}) copy-start(bf16[3,192,192]{2,1,0:T(8,128)(2,1)} %param.19) | copy-start | bytes 663556
  208.9 1.1 copy-start.3
  209.9 1.0 copy-start.2
  210.0 1.9 copy-start.5
  211.0 1.6 copy-start.1
  211.0 2.3 %copy-start = (f32[192,1024]{1,0:T(8,128)S(1)}, f32[192,1024]{1,0:T(8,128)}, u32[]{:S(2)}) copy-start(f32[192,1024]{1,0:T(8,128)} %get-tuple-element.79) | copy-start | bytes 2359300

commit v3 on v2

--- a/solution.py
+++ b/solution.py
@@ -311,8 +311,8 @@
 LANES = 128
 WQ = 3 * WIDTH
 VMEM_LIMIT = 67043328
-REMOTES = 144
-LOCALS = 40
+REMOTES = 208
+LOCALS = 48
 FACTOR = HEAD_DIM ** (-0.5)
 ANY = pl.BlockSpec(memory_space=pl.ANY)
 GAIN1, BIAS1, OUT_BIAS, GAIN2, BIAS2, FC_BIAS, QKV_BIAS, PROJ_BIAS = range(8)
@@ -575,31 +575,51 @@
 
 
 class WeightGather:
-    def __init__(self, links, stage, moved, target):
+    def __init__(self, links, stage, moved, target, pieces=1):
         self.links, self.moved, self.target = links, moved, target
         r, c = links.r, links.c
         self.mine = links.half()
         self.goal = links.crossing(r, c)
-        self.turn = Move(links, self.goal == c, stage, moved, (links.d, r, self.goal))
+        size = HALF // pieces
+        self.local_rows = [pl.ds(i * size, size) for i in range(pieces)]
+        start = links.d * HALF
+        self.rows = [pl.ds(pl.multiple_of(start + i * size, 16), size) for i in range(pieces)]
+        device = (links.d, r, self.goal)
+        self.turns = [
+            Move(links, self.goal == c, stage.at[rows], moved.at[rows], device)
+            for rows in self.local_rows
+        ]
 
     def hop(self):
         links = self.links
-        self.turn.wait()
-        block = self.target.at[links.r, self.mine]
         device = (links.d, self.goal, links.c)
-        self.turn = Move(links, self.goal == links.r, self.moved, block, device)
-
-    def block_of(self, place):
-        return self.target.at[self.links.crossing(self.links.r, place), self.mine]
+        for i, rows in enumerate(self.local_rows):
+            self.turns[i].wait()
+            block = self.target.at[links.r, self.rows[i]]
+            self.turns[i] = Move(links, self.goal == links.r, self.moved.at[rows], block, device)
+
+    def begin(self):
+        links = self.links
+
+        def block_of(rows):
+            return lambda place: self.target.at[links.crossing(links.r, place), rows]
+
+        self.ways = []
+        for turn, rows in zip(self.turns, self.rows):
+            turn.wait()
+            self.ways.append(Line(links, block_of(rows)))
+            self.ways[-1].step(0)
 
     def line(self, t):
         if t == 0:
-            self.turn.wait()
-            self.way = Line(self.links, self.block_of)
-        self.way.step(t)
+            self.begin()
+        else:
+            for way in self.ways:
+                way.step(t)
 
     def share(self):
-        self.way.finish()
+        for way in self.ways:
+            way.finish()
         block = self.target.at[:, self.mine]
         self.shared = self.links.send(block, block, self.links.partner())
 
@@ -613,17 +633,13 @@
         self.mine = links.half()
         self.plane = PlaneGather(links, target.at[:, links.c, self.mine])
 
-    def block_of(self, place):
-        return self.target.at[:, place, self.mine]
-
-    def line(self, t):
-        if t == 0:
-            self.plane.finish()
-            self.way = Line(self.links, self.block_of)
-        self.way.step(t)
+    def begin(self):
+        self.plane.finish()
+        self.ways = [Line(self.links, lambda place: self.target.at[:, place, self.mine])]
+        self.ways[0].step(0)
 
     def share(self):
-        self.way.finish()
+        self.ways[0].finish()
         block = self.target.at[:, :, self.mine]
         self.shared = self.links.send(block, block, self.links.partner())
 
@@ -653,25 +669,23 @@
         self.rise = [Ticket(links, (links.d, links.r, lax.rem(c + 1, 4))) for _ in range(3)]
         self.fall = [Ticket(links, (links.d, links.r, lax.rem(c + 3, 4))) for _ in range(3)]
 
-    def step(self, i):
+    def step(self, t):
         c = self.links.c
-        goal = 3 - i
-        slot = self.up.at[goal - 1]
-        self.pass_on(self.rise[goal - 1], slot, goal, c == 0, jnp.logical_and(c > 0, c < goal))
-        goal = i
-        slot = self.down.at[goal]
-        self.pass_on(self.fall[goal], slot, goal, c == 3, jnp.logical_and(c < 3, c > goal))
-
-    def pass_on(self, ticket, slot, goal, begins, adds):
-        @pl.when(begins)
+        for i in range(t + 1):
+            goal = 3 - t + i
+            self.pass_on(c == i, self.rise[goal - 1], self.up.at[goal - 1], goal, i > 0)
+            goal = t - i
+            self.pass_on(c == 3 - i, self.fall[goal], self.down.at[goal], goal, i > 0)
+
+    def pass_on(self, here, ticket, slot, goal, adds):
+        @pl.when(here)
         def _():
-            ticket(self.block_of(goal), slot).start()
-
-        @pl.when(adds)
-        def _():
-            ticket(slot, slot).wait_recv()
-            add_blocks(slot, [slot, self.block_of(goal)])
-            ticket(slot, slot).start()
+            if adds:
+                ticket(slot, slot).wait_recv()
+                add_blocks(slot, [slot, self.block_of(goal)])
+                ticket(slot, slot).start()
+            else:
+                ticket(self.block_of(goal), slot).start()
 
     def total(self, target):
         c = self.links.c
@@ -703,39 +717,65 @@
 
 
 class WeightReduce:
-    def __init__(self, links, grad, near, sums, up, down, fin, moved, arrived, result):
+    def __init__(self, links, grad, near, sums, up, down, fin, moved, arrived, result, pieces=1):
         self.links, self.grad, self.near, self.sums = links, grad, near, sums
         self.up, self.down, self.fin = up, down, fin
         self.moved, self.arrived, self.result = moved, arrived, result
-        self.to_near = links.send(grad.at[:, links.half(False)], near, links.partner())
-
-    def block_of(self, place):
-        return self.sums.at[self.links.crossing(self.links.r, place)]
+        size = HALF // pieces
+        self.rows = [pl.ds(i * size, size) for i in range(pieces)]
+        self.to_near = [self.send_near(i * size, size) for i in range(pieces)]
+
+    def send_near(self, first, size):
+        links = self.links
+        other = pl.ds(pl.multiple_of((1 - links.d) * HALF + first, 16), size)
+        rows = pl.ds(first, size)
+        return links.send(self.grad.at[:, other], self.near.at[:, rows], links.partner())
 
     def add_near(self):
-        mine = self.links.half()
-        self.to_near.wait()
-        each(4, lambda b: add_rows(self.sums.at[b], [self.grad.at[b, mine], self.near.at[b]]))
-        self.way = LineReduce(self.links, self.block_of, self.up, self.down)
+        links = self.links
+
+        def block_of(rows):
+            return lambda place: self.sums.at[links.crossing(links.r, place), rows]
+
+        self.ways = []
+        for copy, rows in zip(self.to_near, self.rows):
+            copy.wait()
+            first = links.d * HALF + rows.start
+            mine = pl.ds(pl.multiple_of(first, 16), rows.size)
+            each(
+                4,
+                lambda b, rows=rows, mine=mine: add_rows(
+                    self.sums.at[b, rows], [self.grad.at[b, mine], self.near.at[b, rows]]
+                ),
+            )
+            up, down = self.up.at[:, rows], self.down.at[:, rows]
+            self.ways.append(LineReduce(links, block_of(rows), up, down))
 
     def line(self, i):
-        self.way.step(i)
+        for way in self.ways:
+            way.step(i)
 
     def hop(self):
         links = self.links
-        self.way.total(self.fin)
         self.goal = links.crossing(links.r, links.c)
         device = (links.d, self.goal, links.c)
-        self.turn = Move(links, self.goal == links.r, self.fin, self.moved, device)
+        self.turns = []
+        for way, rows in zip(self.ways, self.rows):
+            way.total(self.fin.at[rows])
+            stays = self.goal == links.r
+            self.turns.append(Move(links, stays, self.fin.at[rows], self.moved.at[rows], device))
 
     def back(self):
         links = self.links
-        self.turn.wait()
         device = (links.d, links.r, self.goal)
-        self.turn = Move(links, self.goal == links.c, self.moved, self.arrived, device)
+        for i, rows in enumerate(self.rows):
+            self.turns[i].wait()
+            stays = self.goal == links.c
+            self.turns[i] = Move(links, stays, self.moved.at[rows], self.arrived.at[rows], device)
 
     def share(self):
-        self.turn.wait()
+        for turn in self.turns:
+            turn.wait()
         self.give(self.arrived)
 
     def give(self, total):
@@ -757,18 +797,17 @@
         self.came, self.arrived, self.result = came, arrived, result
         self.to_near = links.send(grad.at[:, :, links.half(False)], near, links.partner())
 
-    def block_of(self, place):
-        return self.sums.at[:, place]
-
     def add_near(self):
         mine = self.links.half()
         self.to_near.wait()
         add_blocks(self.sums, [self.grad.at[:, :, mine], self.near])
-        self.way = LineReduce(self.links, self.block_of, self.up, self.down)
+        self.ways = [
+            LineReduce(self.links, lambda place: self.sums.at[:, place], self.up, self.down)
+        ]
 
     def hop(self):
         links = self.links
-        self.way.total(self.fin)
+        self.ways[0].total(self.fin)
         self.crossing = [
             links.send(self.fin.at[links.across(k)], self.came.at[k - 1], links.plane(k))
             for k in (3, 1, 2)
@@ -907,29 +946,27 @@
     r, c = links.r, links.c
     mine = links.half()
     own = aligned(r * QUARTER, QUARTER)
-    staged = [
-        links.local(tok, xt.at[r]),
-        links.local(wq_in.at[mine], zq),
-        links.local(pre, pres.at[r]),
-        links.local(cols_in, cols),
-        links.local(wo_in.at[mine], woa.at[r, c, mine]),
-        links.local(wf_in.at[mine], zf),
-        links.local(wp_in.at[mine], zp),
-        links.local(cot, gt.at[r]),
-    ]
+    first = [links.local(wq_in.at[mine], zq), links.local(tok, xt.at[r])]
+    first += [links.local(pre, pres.at[r]), links.local(wo_in.at[mine], woa.at[r, c, mine])]
+    then = [links.local(wf_in.at[mine], zf), links.local(wp_in.at[mine], zp)]
+    then += [links.local(cols_in, cols), links.local(cot, gt.at[r])]
     links.meet(
         links.partner(), *(links.plane(k) for k in (1, 2, 3)), *(links.column(k) for k in (1, 2, 3))
     )
-    for copy in staged:
+    for copy in first:
         copy.wait()
 
-    get_q = WeightGather(links, zq, mq, wqa)
+    get_q = WeightGather(links, zq, mq, wqa, 3)
     tokens = PlaneGather(links, xt)
     prefixes = [links.send(pres.at[r], pres.at[r], links.plane(k)) for k in (1, 2, 3)]
     get_o = SquareGather(links, woa)
+    for copy in then:
+        copy.wait()
     for j in range(7):
         colb[j] = jnp.broadcast_to(cols[:, j : j + 1], (D, LANES))
     get_q.hop()
+    get_f = WeightGather(links, zf, mf, wfa)
+    get_p = WeightGather(links, zp, mp, wpa)
     get_o.plane.relay()
     get_q.line(0)
     tokens.relay()
@@ -945,8 +982,9 @@
     )
     for copy in prefixes:
         copy.wait()
+    get_f.hop()
+    get_p.hop()
     get_o.line(1)
-    get_f = WeightGather(links, zf, mf, wfa)
     get_q.finish()
 
     def project(b):
@@ -963,6 +1001,11 @@
 
     def get_attn(rows, lanes):
         return at[r, rows, lanes]
+
+    attns = []
+
+    def gather_head(h):
+        attns.append(PlaneGather(links, at.at[:, h * HEAD_DIM : (h + 1) * HEAD_DIM]))
 
     attend(
         qkv,
@@ -970,24 +1013,25 @@
         put_attn,
         lse,
         [
-            in_turn(lambda: get_o.line(2), get_f.hop),
-            in_turn(lambda: get_o.line(3), lambda: get_f.line(0), grads.relay),
-            lambda: get_f.line(1),
+            in_turn(lambda: get_o.line(2), lambda: get_f.line(0)),
+            in_turn(lambda: gather_head(0), lambda: get_o.line(3), lambda: get_f.line(1)),
+            in_turn(
+                lambda: gather_head(1), get_o.share, grads.relay, lambda: attns[0].relay(),
+                lambda: get_f.line(2), lambda: get_p.line(0),
+            ),
         ],
     )
-    attns = PlaneGather(links, at)
-    get_p = WeightGather(links, zp, mp, wpa)
-    get_o.share()
-    get_f.line(2)
-    get_p.hop()
+    gather_head(2)
+    attns[1].relay()
     get_f.line(3)
     get_f.share()
-    get_p.line(0)
-    attns.relay()
+    get_p.line(1)
+    attns[2].relay()
+    get_p.line(2)
     get_o.finish()
     grads.finish()
-    get_p.line(1)
-    attns.finish()
+    for attn in attns:
+        attn.finish()
 
     def join(i):
         b, lanes = lax.div(i, 4), aligned(lax.rem(i, 4) * QUARTER, QUARTER)
@@ -997,10 +1041,9 @@
         mid[rows, lanes] = wide(xt[b, :, lanes]) + (value + jnp.concatenate([bias, bias], axis=1))
 
     each(16, join)
-    get_p.line(2)
-    normalize(lambda lanes: mid[:, lanes], sn, st2, colb.at[GAIN2], colb.at[BIAS2])
     get_p.line(3)
     get_p.share()
+    normalize(lambda lanes: mid[:, lanes], sn, st2, colb.at[GAIN2], colb.at[BIAS2])
     get_f.finish()
 
     def up(b):
@@ -1032,9 +1075,9 @@
 
     each(4, proj_grads)
     put_p = WeightReduce(links, gp, near_p, sum_p, up_p, dn_p, fin_p, hop_p, got_p, wp_hbm)
-    seconds.relay()
     each(4, fc_grads)
     put_f = WeightReduce(links, gf, near_f, sum_f, up_f, dn_f, fin_f, hop_f, got_f, wf_hbm)
+    seconds.relay()
     put_p.add_near()
     put_p.line(0)
 
@@ -1052,9 +1095,8 @@
         lanes = slice(b * QUARTER, (b + 1) * QUARTER)
         total = total + jnp.sum(wide(hg[:, lanes]), axis=1, keepdims=True)
     vcol[...] = jnp.where(lane == V_FC + r, total, 0.0)
+    put_f.add_near()
     put_p.line(1)
-    put_f.add_near()
-    put_p.line(2)
     put_f.line(0)
     seconds.finish()
 
@@ -1097,9 +1139,8 @@
 
     each(4, square_grads)
     put_o = SquareReduce(links, sq, near_o, sum_o, up_o, dn_o, fin_o, hop_o, got_o, wo_hbm)
-    put_p.hop()
+    put_p.line(2)
     put_f.line(1)
-    put_f.line(2)
     put_o.add_near()
     for copy in turns:
         copy.wait()
@@ -1108,9 +1149,9 @@
     attend_back(
         qkv, limit_value, get_attn, lse, dout, dqkv, ksum, vsum,
         [
-            in_turn(put_p.back, lambda: put_o.line(0)),
-            in_turn(put_f.hop, lambda: put_o.line(1)),
-            in_turn(outs.relay, put_p.share, lambda: put_o.line(2)),
+            in_turn(put_p.hop, lambda: put_f.line(2)),
+            in_turn(put_p.back, put_f.hop, lambda: put_o.line(0)),
+            in_turn(outs.relay, put_p.share, put_f.back, lambda: put_o.line(1)),
         ],
     )
 
@@ -1118,7 +1159,7 @@
         gq[b] = low(dot(fn[aligned(b * WIDTH, WIDTH), :], dqkv[...], 1, 1))
 
     each(4, query_grads)
-    put_q = WeightReduce(links, gq, near_q, sum_q, up_q, dn_q, fin_q, hop_q, got_q, wq_hbm)
+    put_q = WeightReduce(links, gq, near_q, sum_q, up_q, dn_q, fin_q, hop_q, got_q, wq_hbm, 3)
 
     stat[...] = jnp.zeros_like(stat)
     firsts = PlaneReduce(links, lambda place: fgp.at[place], WIDTH, x1, y1, z1)
@@ -1149,12 +1190,14 @@
         if k == 3:
             put_q.add_near()
             put_q.line(0)
+        elif k == 1:
+            put_o.line(2)
+            put_q.line(1)
         elif k == 2:
-            put_q.line(1)
+            put_f.share()
+            put_q.line(2)
+            firsts.relay()
     stat_sends = [links.send(stat, stat_in.at[k - 1], links.plane(k)) for k in (1, 2, 3)]
-    put_q.line(2)
-    firsts.relay()
-    put_f.back()
     put_o.hop()
     rows = aligned(r * WIDTH, WIDTH)
     spot = lane[:WIDTH]
@@ -1172,10 +1215,9 @@
     vec_near.wait()
     vec[1] = vec[0] + vec_in[0]
     vec_plane = [links.send(vec.at[1], vec_in.at[k], links.plane(k)) for k in (1, 2, 3)]
-    put_f.share()
     put_o.back()
+    put_o.share()
     put_q.back()
-    put_o.share()
     for copy in vec_plane:
         copy.wait()
     vec[2] = vec[1] + vec_in[1] + vec_in[2] + vec_in[3]

time: 215 us -> 175 us (0.81)
  Pallas kernels: 194 us -> 154 us
    pallas_call x1, Pallas kernels: 194 us -> 154 us  [run_block(): pl.pallas_call(block_kernel, out_shape=[jax.ShapeDtypeStruct(*result) for...]
where the time goes in v3:
time: 175 us; the launch traced here: 174 us
  Pallas kernels  154 us (88%)
  local copies, waits for them, and re-layouts  16.8 us (10%)
  other arithmetic  2.48 us (1%)
    pallas_call x1, Pallas kernels, run_block(): pl.pallas_call(block_kernel, out_shape=[jax.ShapeDtypeStruct(*result) for...  154 us
    another operation x10, local copies, waits for them, and re-layouts, plane_device(): jnp.stack([ln1_gain, ln1_bias, out_bias, ln2_gain, ln2_bias, take_portion...  5.11 us

profile of v3, /device:TPU:0, one launch (start us, length us, event | category | flops | bytes accessed | tf_op | source)
XLA Modules:
  0.0 174.5 jit_solution(828915109037140865)
XLA Ops:
  0.6 0.0 copy-start.4
  0.7 0.8 constant_dynamic-slice_fusion
  1.5 0.1 pad_maximum_fusion
  1.6 0.8 dynamic_slice.6
  2.4 0.7 stack.27
  3.1 0.7 stack.28
  3.7 0.7 stack.29
  4.4 0.7 stack.30
  5.1 0.7 stack.31
  5.8 0.7 stack.34
  6.6 0.9 copy.45.cols_in
  7.5 0.0 copy-done.4
  7.5 0.2 copy.43
  7.6 0.9 copy.44.wq_in
  9.1 0.6 broadcast_in_dim.12.pre
  9.7 153.9 %block.1 = (bf16[192,1024]{1,0:T(8,128)(2,1)}, f32[192,1024]{1,0:T(8,128)}, bf16[192,576]{1,0:T(8,128)(2,1)}, bf16[192,768]{1,0:T(8,128)(2,1)}, bf16[192,768]{1,...) custom-call(bf16[192,1024]{1,0:T(8,128)(2,1)} %tok.1, bf16[192,1024]{1,0:T(8,128)(2,1)} %cot.1, ...), custom_call_target="tpu_custom_call" | custom-call | tf_op jit(solution)/shard_map/block/pallas_call | solution.py:1301
  163.6 1.8 %slice_reduce_fusion = (f32[768]{0:T(1024)}, f32[768]{0:T(1024)}, f32[768]{0:T(1024)}, f32[768]{0:T(1024)}, f32[768]{0:T(1024)}, /*index=5*/f32[768]{0:T(1024)}) fusion(f32[16,768]{1,0:T(8,128)} %get-tuple-element.23), kind=kLoop, calls=%fused_computation.1 | loop fusion | bytes 36864 | tf_op jit(solution)/shard_map/slice | solution.py:1353
  165.4 0.7 slice.38
  166.1 0.6 reshape.39
  166.7 1.3 slice.34
  168.1 1.1 copy.46
  169.2 0.0 copy-start.3
  169.2 1.1 copy.47
  170.3 0.0 copy-done.3
  170.3 0.0 copy-start.2
  170.3 0.0 copy-start.5
  170.3 0.9 convert_element_type.22
  171.1 0.2 copy-done.2
  171.3 0.0 copy-start.1
  171.3 0.0 copy-start
  171.3 0.9 convert_element_type.23
  172.2 0.0 copy-done.5
  172.2 0.7 convert_element_type.21
  172.8 0.0 copy-done.1
  172.8 0.7 copy.51
  173.6 0.0 copy-done
  173.6 0.9 copy.52
  (4 shorter events, 0.1 us)
Async XLA Ops:
  0.6 6.8 %copy-start.4 = (bf16[3,192,192]{2,1,0:T(8,128)(2,1)S(1)}, bf16[3,192,192]{2,1,0:T(8,128)(2,1)}, u32[]{:S(2)}) copy-start(bf16[3,192,192]{2,1,0:T(8,128)(2,1)} %param.19) | copy-start | bytes 663556
  169.2 1.1 copy-start.3
  170.3 1.0 copy-start.2
  170.3 1.9 %copy-start.5 = (bf16[192,192]{1,0:T(8,128)(2,1)S(1)}, bf16[192,192]{1,0:T(8,128)(2,1)}, u32[]{:S(2)}) copy-start(bf16[192,192]{1,0:T(8,128)(2,1)} %get-tuple-element.25) | copy-start | bytes 221188
  171.3 1.6 copy-start.1
  171.3 2.3 %copy-start = (f32[192,1024]{1,0:T(8,128)S(1)}, f32[192,1024]{1,0:T(8,128)}, u32[]{:S(2)}) copy-start(f32[192,1024]{1,0:T(8,128)} %get-tuple-element.79) | copy-start | bytes 2359300

commit v4 on v3

--- a/solution.py
+++ b/solution.py
@@ -312,10 +312,10 @@
 WQ = 3 * WIDTH
 VMEM_LIMIT = 67043328
 REMOTES = 208
-LOCALS = 48
+LOCALS = 64
 FACTOR = HEAD_DIM ** (-0.5)
 ANY = pl.BlockSpec(memory_space=pl.ANY)
-GAIN1, BIAS1, OUT_BIAS, GAIN2, BIAS2, FC_BIAS, QKV_BIAS, PROJ_BIAS = range(8)
+GAIN1, BIAS1, OUT_BIAS, GAIN2, BIAS2, PROJ_BIAS, Q_BIAS, V_BIAS, FC_BIAS = range(9)
 V_GAIN1, V_BIAS1, V_QUERY, V_VALUE, V_OUT, V_GAIN2, V_BIAS2, V_PROJ, V_FC = range(9)
 CENTER, INVERSE = range(2)
 
@@ -385,11 +385,16 @@
         low_bit = lax.rem(lax.rem(row, 2) + lax.rem(place, 2), 2)
         return low_bit + 2 * lax.rem(lax.div(row, 2) + lax.div(place, 2), 2)
 
-    def meet(self, *devices):
+    def greet(self):
+        devices = [self.partner(), *(self.plane(k) for k in (1, 2, 3))]
+        devices += [self.column(k) for k in (1, 2, 3)]
         barrier = pltpu.get_barrier_semaphore()
         for device in devices:
             pl.semaphore_signal(barrier, 1, device_id=device, device_id_type=MESH)
-        pl.semaphore_wait(barrier, len(devices))
+        self.greeted = len(devices)
+
+    def meet(self):
+        pl.semaphore_wait(pltpu.get_barrier_semaphore(), self.greeted)
 
     def send(self, source, target, device):
         place = self.remotes
@@ -458,13 +463,19 @@
 
 
 class PlaneGather:
-    def __init__(self, links, target):
+    def __init__(self, links, target, in_parts=False):
         self.links, self.target = links, target
         rows = target.shape[1] // 2
         self.low, self.high = pl.ds(0, rows), pl.ds(rows, rows)
         first, second = target.at[links.r, self.low], target.at[links.r, self.high]
         self.x_low = links.send(first, first, links.plane(1))
         self.y_high = links.send(second, second, links.plane(2))
+        if not in_parts:
+            self.rest()
+
+    def rest(self):
+        links, target = self.links, self.target
+        first, second = target.at[links.r, self.low], target.at[links.r, self.high]
         self.x_high = links.send(second, second, links.plane(1))
         self.y_low = links.send(first, first, links.plane(2))
 
@@ -860,8 +871,9 @@
 
 def attend(qkv, limit_value, attn_of, log_total, between):
     def head(h):
-        between[h]()
         for block in range(4):
+            for action in between.get(h * 4 + block, ()):
+                action()
             last, _ = key_span(block)
             lanes = slice(block * QUARTER, (block + 1) * QUARTER)
             queries = qkv[head_rows(h, 0), lanes] * jnp.bfloat16(FACTOR)
@@ -882,8 +894,9 @@
     qkv, limit_value, attn_of, log_total, out_grad, qkv_grad, key_sum, value_sum, between
 ):
     def head(h):
-        between[h]()
         for block in (3, 2, 1, 0):
+            for action in between.get(h * 4 + 3 - block, ()):
+                action()
             last, _ = key_span(block)
             lanes = slice(block * QUARTER, (block + 1) * QUARTER)
             queries = qkv[head_rows(h, 0), lanes] * jnp.bfloat16(FACTOR)
@@ -922,18 +935,11 @@
     return u * shared, derivative
 
 
-def in_turn(*actions):
-    def run():
-        for action in actions:
-            action()
-
-    return run
-
-
 def block_kernel(
-    tok, cot, pre, wq_in, wf_in, wp_in, wo_in, cols_in,
+    limit, tok, gain1_in, bias1_in, wq_in, qv_in, wo_in, out_in, gain2_in, bias2_in,
+    wf_in, fc_in, wp_in, proj_in, cot,
     out_hbm, grad_hbm, wq_hbm, wf_hbm, wp_hbm, wo_hbm, vec_hbm,
-    xt, gt, wqa, wfa, wpa, woa, zq, zf, zp, mq, mf, mp, pres, cols, colb,
+    rows1, qv, fc, wq_here, xt, gt, wqa, wfa, wpa, woa, zq, zf, zp, mq, mf, mp, pres, colb,
     fn, qkv, at, lse, st1, st2, mid, sn, act, slope, op, hg, sp,
     x2, y2, z2, x_out, y_out, z_out, x1, y1, z1, br, ap, dout, brf, dqkv, ksum, vsum,
     gf, gp, gq, near_f, near_p, near_q, sum_f, sum_p, sum_q, up_f, up_p, up_q, dn_f, dn_p, dn_q,
@@ -946,50 +952,66 @@
     r, c = links.r, links.c
     mine = links.half()
     own = aligned(r * QUARTER, QUARTER)
-    first = [links.local(wq_in.at[mine], zq), links.local(tok, xt.at[r])]
-    first += [links.local(pre, pres.at[r]), links.local(wo_in.at[mine], woa.at[r, c, mine])]
+    links.greet()
+    singles = (gain1_in, bias1_in, out_in, gain2_in, bias2_in, proj_in)
+    first = [links.local(wq_in.at[:, mine], wq_here), links.local(tok, xt.at[r])]
+    first += [links.local(source, rows1.at[i]) for i, source in enumerate(singles)]
+    first += [links.local(qv_in, qv), links.local(fc_in, fc)]
     then = [links.local(wf_in.at[mine], zf), links.local(wp_in.at[mine], zp)]
-    then += [links.local(cols_in, cols), links.local(cot, gt.at[r])]
-    links.meet(
-        links.partner(), *(links.plane(k) for k in (1, 2, 3)), *(links.column(k) for k in (1, 2, 3))
-    )
+    then += [links.local(wo_in.at[mine], woa.at[r, c, mine]), links.local(cot, gt.at[r])]
     for copy in first:
         copy.wait()
+    zq[...] = jnp.concatenate([wq_here[i] for i in range(3)], axis=1)
+    pres[r] = jnp.full((8, LANES), limit[0], jnp.int32)
+
+    def column(kind, place, values):
+        spread = jnp.broadcast_to(values[None, :], (LANES, LANES))
+        colb[kind, pl.ds(place * LANES, LANES)] = spread.T
+
+    for place in range(D // LANES):
+        part = pl.ds(place * LANES, LANES)
+        for kind in range(len(singles)):
+            column(kind, place, rows1[kind, part])
+        column(Q_BIAS, place, qv[0, part])
+        column(V_BIAS, place, qv[1, part])
+        column(FC_BIAS, place, fc[pl.ds(pl.multiple_of(r * D + place * LANES, LANES), LANES)])
+    links.meet()
 
     get_q = WeightGather(links, zq, mq, wqa, 3)
-    tokens = PlaneGather(links, xt)
-    prefixes = [links.send(pres.at[r], pres.at[r], links.plane(k)) for k in (1, 2, 3)]
-    get_o = SquareGather(links, woa)
+    tokens = PlaneGather(links, xt, in_parts=True)
     for copy in then:
         copy.wait()
-    for j in range(7):
-        colb[j] = jnp.broadcast_to(cols[:, j : j + 1], (D, LANES))
     get_q.hop()
+    tokens.rest()
     get_f = WeightGather(links, zf, mf, wfa)
+    prefixes = [links.send(pres.at[r], pres.at[r], links.plane(k)) for k in (1, 2, 3)]
+    get_q.line(0)
+    tokens.relay()
+    get_o = SquareGather(links, woa)
+    get_q.line(1)
     get_p = WeightGather(links, zp, mp, wpa)
     get_o.plane.relay()
-    get_q.line(0)
-    tokens.relay()
-    get_q.line(1)
     get_q.line(2)
     get_o.line(0)
     get_q.line(3)
     get_q.share()
     tokens.finish()
     grads = PlaneGather(links, gt)
+    get_f.hop()
+    get_p.hop()
     normalize(
         lambda lanes: wide(merged(xt[:, :, lanes])), fn, st1, colb.at[GAIN1], colb.at[BIAS1]
     )
     for copy in prefixes:
         copy.wait()
-    get_f.hop()
-    get_p.hop()
-    get_o.line(1)
     get_q.finish()
+    head_bias = aligned(r * WIDTH, WIDTH)
 
     def project(b):
         lanes = aligned(b * QUARTER, QUARTER)
-        bias = colb[QKV_BIAS, :WQ]
+        nothing = jnp.zeros((WIDTH, LANES), jnp.float32)
+        bias = [colb[Q_BIAS, head_bias], nothing, colb[V_BIAS, head_bias]]
+        bias = jnp.concatenate(bias, axis=0)
         value = dot(merged(wqa[...]), fn[:, lanes], 0, 0)
         qkv[:, lanes] = low(value + jnp.concatenate([bias, bias], axis=1))
 
@@ -1012,24 +1034,26 @@
         limit_value,
         put_attn,
         lse,
-        [
-            in_turn(lambda: get_o.line(2), lambda: get_f.line(0)),
-            in_turn(lambda: gather_head(0), lambda: get_o.line(3), lambda: get_f.line(1)),
-            in_turn(
-                lambda: gather_head(1), get_o.share, grads.relay, lambda: attns[0].relay(),
-                lambda: get_f.line(2), lambda: get_p.line(0),
-            ),
-        ],
+        {
+            0: [lambda: get_o.line(1)],
+            3: [lambda: get_f.line(0)],
+            4: [lambda: gather_head(0), grads.relay],
+            7: [lambda: get_o.line(2)],
+            8: [lambda: gather_head(1), lambda: attns[0].relay()],
+            10: [lambda: get_f.line(1)],
+        },
     )
     gather_head(2)
     attns[1].relay()
+    get_o.line(3)
+    get_o.share()
+    get_f.line(2)
+    get_p.line(0)
+    attns[2].relay()
     get_f.line(3)
     get_f.share()
     get_p.line(1)
-    attns[2].relay()
-    get_p.line(2)
     get_o.finish()
-    grads.finish()
     for attn in attns:
         attn.finish()
 
@@ -1041,8 +1065,7 @@
         mid[rows, lanes] = wide(xt[b, :, lanes]) + (value + jnp.concatenate([bias, bias], axis=1))
 
     each(16, join)
-    get_p.line(3)
-    get_p.share()
+    get_p.line(2)
     normalize(lambda lanes: mid[:, lanes], sn, st2, colb.at[GAIN2], colb.at[BIAS2])
     get_f.finish()
 
@@ -1054,7 +1077,17 @@
         act[:, lanes] = low(value)
         slope[:, lanes] = derivative
 
-    each(4, up)
+    each(2, up)
+    get_p.line(3)
+    get_p.share()
+    each(2, lambda b: up(b + 2))
+    grads.finish()
+
+    def proj_grads(b):
+        gp[b] = low(dot(gt[b], act[...], 1, 1))
+
+    each(4, proj_grads)
+    put_p = WeightReduce(links, gp, near_p, sum_p, up_p, dn_p, fin_p, hop_p, got_p, wp_hbm)
     get_p.finish()
 
     seconds = PlaneReduce(
@@ -1066,20 +1099,17 @@
         hg[:, lanes] = low(value * slope[:, lanes])
         sp[:, lanes] = low(dot(merged(wfa[...]), hg[:, lanes], 1, 0))
         seconds.give(k)
-
-    def proj_grads(b):
-        gp[b] = low(dot(gt[b], act[...], 1, 1))
+        if k == 3:
+            put_p.add_near()
+            put_p.line(0)
 
     def fc_grads(b):
         gf[b] = low(dot(sn[aligned(b * WIDTH, WIDTH), :], hg[...], 1, 1))
 
-    each(4, proj_grads)
-    put_p = WeightReduce(links, gp, near_p, sum_p, up_p, dn_p, fin_p, hop_p, got_p, wp_hbm)
     each(4, fc_grads)
     put_f = WeightReduce(links, gf, near_f, sum_f, up_f, dn_f, fin_f, hop_f, got_f, wf_hbm)
     seconds.relay()
-    put_p.add_near()
-    put_p.line(0)
+    put_p.line(1)
 
     def down(b):
         lanes = aligned(b * QUARTER, QUARTER)
@@ -1088,16 +1118,15 @@
 
     each(4, down)
     outs = PlaneReduce(links, lambda place: op.at[place], WIDTH, x_out, y_out, z_out)
-
+    put_f.add_near()
+    put_f.line(0)
     lane = lax.broadcasted_iota(jnp.int32, (D, LANES), 1)
     total = jnp.zeros((D, 1), jnp.float32)
     for b in range(4):
         lanes = slice(b * QUARTER, (b + 1) * QUARTER)
         total = total + jnp.sum(wide(hg[:, lanes]), axis=1, keepdims=True)
     vcol[...] = jnp.where(lane == V_FC + r, total, 0.0)
-    put_f.add_near()
-    put_p.line(1)
-    put_f.line(0)
+    put_p.line(2)
     seconds.finish()
 
     def back(j):
@@ -1139,20 +1168,24 @@
 
     each(4, square_grads)
     put_o = SquareReduce(links, sq, near_o, sum_o, up_o, dn_o, fin_o, hop_o, got_o, wo_hbm)
-    put_p.line(2)
     put_f.line(1)
     put_o.add_near()
+    put_p.hop()
     for copy in turns:
         copy.wait()
     for k in (3, 1, 2):
         outs.give(k)
     attend_back(
         qkv, limit_value, get_attn, lse, dout, dqkv, ksum, vsum,
-        [
-            in_turn(put_p.hop, lambda: put_f.line(2)),
-            in_turn(put_p.back, put_f.hop, lambda: put_o.line(0)),
-            in_turn(outs.relay, put_p.share, put_f.back, lambda: put_o.line(1)),
-        ],
+        {
+            1: [lambda: put_o.line(0)],
+            2: [lambda: put_f.line(2)],
+            4: [put_p.back],
+            5: [outs.relay],
+            7: [lambda: put_o.line(1)],
+            9: [put_f.hop, put_p.share],
+            11: [lambda: put_o.line(2)],
+        },
     )
 
     def query_grads(b):
@@ -1191,13 +1224,12 @@
             put_q.add_near()
             put_q.line(0)
         elif k == 1:
-            put_o.line(2)
+            put_f.back()
+        elif k == 2:
             put_q.line(1)
-        elif k == 2:
-            put_f.share()
-            put_q.line(2)
             firsts.relay()
     stat_sends = [links.send(stat, stat_in.at[k - 1], links.plane(k)) for k in (1, 2, 3)]
+    put_q.line(2)
     put_o.hop()
     rows = aligned(r * WIDTH, WIDTH)
     spot = lane[:WIDTH]
@@ -1211,6 +1243,7 @@
     vcol[rows, :] = vcol[rows, :] + add
     vec[0] = vcol[...].T[:16]
     vec_near = links.send(vec.at[0], vec_in.at[0], links.partner())
+    put_f.share()
     put_q.hop()
     vec_near.wait()
     vec[1] = vec[0] + vec_in[0]
@@ -1226,7 +1259,7 @@
 
     def last_out(j):
         lanes = aligned(j * LANES, LANES)
-        value = mid[rows, lanes] + cols[rows, PROJ_BIAS : PROJ_BIAS + 1] + outs.total(lanes)
+        value = mid[rows, lanes] + colb[PROJ_BIAS, rows] + outs.total(lanes)
         out_v[:, lanes] = low(value)
 
     each(LEN // LANES, last_out)
@@ -1268,12 +1301,13 @@
         return [vmem((2, rows // 2, lanes), narrow) for _ in range(3)]
 
     scratch = [
+        vmem((6, D), full), vmem((2, D), full), vmem((FF,), full), vmem((3, HALF, WIDTH), narrow),
         vmem(sequence, narrow), vmem(sequence, narrow),
         vmem((4, WIDTH, WQ), narrow), vmem((4, WIDTH, D), narrow), vmem((4, WIDTH, D), narrow),
         vmem((4, 4, WIDTH, WIDTH), narrow),
         vmem((HALF, WQ), narrow), vmem((HALF, D), narrow), vmem((HALF, D), narrow),
         vmem((HALF, WQ), narrow), vmem((HALF, D), narrow), vmem((HALF, D), narrow),
-        vmem((4, 8, LANES), jnp.int32), vmem((D, 8), full), vmem((7, D, LANES), full),
+        vmem((4, 8, LANES), jnp.int32), vmem((9, D, LANES), full),
         vmem(tall, narrow), vmem((WQ, LEN), narrow), vmem(sequence, narrow),
         vmem((8, LEN), full), vmem((8, LEN), full), vmem((8, LEN), full),
         vmem(tall, full), vmem(tall, narrow), vmem(tall, narrow), vmem(tall, full),
@@ -1301,7 +1335,7 @@
     return pl.pallas_call(
         block_kernel,
         out_shape=[jax.ShapeDtypeStruct(*result) for result in results],
-        in_specs=[ANY] * len(arguments),
+        in_specs=[pl.BlockSpec(memory_space=pltpu.SMEM)] + [ANY] * (len(arguments) - 1),
         out_specs=[ANY] * len(results),
         scratch_shapes=scratch,
         compiler_params=pltpu.CompilerParams(
@@ -1311,47 +1345,47 @@
     )(*arguments)
 
 
+def finish_kernel(
+    out, grad, wq, wf, wp, wo, vec,
+    out_done, grad_done, gain1, bias1, wq_done, qv, wo_done, out_bias, gain2, bias2,
+    wf_done, fc, wp_done, proj,
+):
+    out_done[...] = out[...]
+    grad_done[...] = grad[...]
+    for i in range(3):
+        wq_done[i] = wide(wq[:, i * WIDTH : (i + 1) * WIDTH])
+    wo_done[...] = wide(wo[...])
+    wf_done[...] = wide(wf[...])
+    wp_done[...] = wide(wp[...])
+    singles = ((gain1, V_GAIN1), (bias1, V_BIAS1), (out_bias, V_OUT), (gain2, V_GAIN2))
+    for target, row in singles + ((bias2, V_BIAS2), (proj, V_PROJ)):
+        target[...] = vec[row]
+    qv[...] = vec[V_QUERY : V_VALUE + 1]
+    for i in range(4):
+        fc[pl.ds(i * D, D)] = vec[V_FC + i]
+
+
 def plane_device(
     tokens, prefix, ln1_gain, ln1_bias, w_qkv, qv_bias, w_out, out_bias,
     ln2_gain, ln2_bias, w_fc, fc_bias, w_proj, proj_bias, cotangent,
 ):
-    r = lax.axis_index("row")
-    bias = take_portion(qv_bias, r, WIDTH, 1)
-    nothing = jnp.zeros((WIDTH,), jnp.float32)
-    bias = jnp.concatenate([bias[0], nothing, bias[1], nothing])
-    columns = jnp.stack(
-        [
-            ln1_gain, ln1_bias, out_bias, ln2_gain, ln2_bias,
-            take_portion(fc_bias, r, D, 0), bias, proj_bias,
-        ],
-        axis=1,
-    )
-    output, input_grad, w_qkv_grad, w_fc_grad, w_proj_grad, w_out_grad, vector = run_block(
-        tokens,
-        cotangent,
-        jnp.broadcast_to(prefix[:, None], (8, LANES)),
-        w_qkv.transpose(1, 0, 2).reshape(WIDTH, WQ),
-        w_fc,
-        w_proj,
-        w_out,
-        columns,
-    )
-    return (
-        output,
-        input_grad,
-        vector[V_GAIN1],
-        vector[V_BIAS1],
-        wide(w_qkv_grad.reshape(WIDTH, 3, WIDTH).transpose(1, 0, 2)),
-        vector[V_QUERY : V_VALUE + 1],
-        wide(w_out_grad),
-        vector[V_OUT],
-        vector[V_GAIN2],
-        vector[V_BIAS2],
-        wide(w_fc_grad),
-        vector[V_FC : V_FC + 4].reshape(FF),
-        wide(w_proj_grad),
-        vector[V_PROJ],
-    )
+    pieces = run_block(
+        prefix, tokens, ln1_gain, ln1_bias, w_qkv, qv_bias, w_out, out_bias,
+        ln2_gain, ln2_bias, w_fc, fc_bias, w_proj, proj_bias, cotangent,
+    )
+    wide_results = [
+        (WIDTH, LEN), (D,), (D,), (3, WIDTH, WIDTH), (2, D), (WIDTH, WIDTH), (D,), (D,), (D,),
+        (WIDTH, D), (FF,), (WIDTH, D), (D,),
+    ]
+    results = [jax.ShapeDtypeStruct((WIDTH, LEN), jnp.bfloat16)]
+    results += [jax.ShapeDtypeStruct(dims, jnp.float32) for dims in wide_results]
+    return pl.pallas_call(
+        finish_kernel,
+        out_shape=results,
+        in_specs=[pl.BlockSpec(memory_space=pltpu.VMEM)] * len(pieces),
+        out_specs=[pl.BlockSpec(memory_space=pltpu.VMEM)] * len(results),
+        name="results",
+    )(*pieces)
 
 
 def solution(mesh):

time: 175 us -> 154 us (0.88)
  local copies, waits for them, and re-layouts: 16.8 us -> 0 us
  other arithmetic: 2.48 us -> 0 us
  Pallas kernels: 154 us -> 152 us
    another operation x10 -> x0, local copies, waits for them, and re-layouts: 5.11 us -> none  [plane_device(): jnp.stack([ln1_gain, ln1_bias, out_bias, ln2_gain, ln2_bias, take_portion...]
    pallas_call x1, Pallas kernels: 154 us -> 149 us  [run_block(): pl.pallas_call(block_kernel, out_shape=[jax.ShapeDtypeStruct(*result) for...]
    slice x4 -> x0, local copies, waits for them, and re-layouts: 4.67 us -> none  [the longest x1 1.75 us: plane_device(): vector[V_PROJ]]
    pallas_call x0 -> x1, Pallas kernels: none -> 3.31 us  [plane_device(): pl.pallas_call(finish_kernel, out_shape=results, in_specs=[pl.BlockSpec(m...]
    unnamed x15 -> x0, local copies, waits for them, and re-layouts: 2.89 us -> none
    convert_element_type x3 -> x0, other arithmetic: 2.4 us -> none  [wide(): return value.astype(jnp.float32)]
where the time goes in v4:
time: 154 us; the launch traced here: 153 us
  Pallas kernels  152 us (99%)
    pallas_call x1, Pallas kernels, run_block(): pl.pallas_call(block_kernel, out_shape=[jax.ShapeDtypeStruct(*result) for...  149 us
    pallas_call x1, Pallas kernels, plane_device(): pl.pallas_call(finish_kernel, out_shape=results, in_specs=[pl.BlockSpec(m...  3.31 us

profile of v4, /device:TPU:0, one launch (start us, length us, event | category | flops | bytes accessed | tf_op | source)
XLA Modules:
  0.0 153.5 jit_solution(12208198151188911497)
XLA Ops:
  1.3 148.8 %block.1 = (bf16[192,1024]{1,0:T(8,128)(2,1)}, f32[192,1024]{1,0:T(8,128)}, bf16[192,576]{1,0:T(8,128)(2,1)}, bf16[192,768]{1,0:T(8,128)(2,1)}, bf16[192,768]{1,...) custom-call(s32[1]{0:T(128)S(6)} %copy.29.limit, bf16[192,1024]{1,0:T(8,128)(2,1)} %tok.1, f32[768]{0:T(1024)} %gain1_in.1, ...), custom_call_target="tpu_custom_call" | custom-call | tf_op jit(solution)/shard_map/block/pallas_call | solution.py:1335
  150.2 3.3 %results.1 = (bf16[192,1024]{1,0:T(8,128)(2,1)}, f32[192,1024]{1,0:T(8,128)}, f32[768]{0:T(1024)}, f32[768]{0:T(1024)}, f32[3,192,192]{2,1,0:T(8,128)}, /*index=...) custom-call(bf16[192,1024]{1,0:T(8,128)(2,1)} %get-tuple-element.21., ...), custom_call_target="tpu_custom_call" | custom-call | tf_op jit(solution)/shard_map/results/pallas_call | solution.py:1382

commit v5 on v4

--- a/solution.py
+++ b/solution.py
@@ -638,21 +638,26 @@
         self.shared.wait()
 
 
-class SquareGather(WeightGather):
+class SquareGather:
     def __init__(self, links, target):
         self.links, self.target = links, target
         self.mine = links.half()
-        self.plane = PlaneGather(links, target.at[:, links.c, self.mine])
-
-    def begin(self):
+        self.way = Line(links, lambda place: target.at[links.r, place, self.mine])
+
+    def line(self, t):
+        self.way.step(t)
+
+    def cross(self):
+        self.way.finish()
+        self.plane = PlaneGather(self.links, self.target.at[:, :, self.mine])
+
+    def share(self):
         self.plane.finish()
-        self.ways = [Line(self.links, lambda place: self.target.at[:, place, self.mine])]
-        self.ways[0].step(0)
-
-    def share(self):
-        self.ways[0].finish()
         block = self.target.at[:, :, self.mine]
         self.shared = self.links.send(block, block, self.links.partner())
+
+    def finish(self):
+        self.shared.wait()
 
 
 def add_rows(target, terms):
@@ -945,7 +950,7 @@
     gf, gp, gq, near_f, near_p, near_q, sum_f, sum_p, sum_q, up_f, up_p, up_q, dn_f, dn_p, dn_q,
     fin_f, fin_p, fin_q, hop_f, hop_p, hop_q, got_f, got_p, got_q,
     sq, near_o, sum_o, up_o, dn_o, fin_o, hop_o, got_o,
-    fgp, vcol, vec, vec_in, stat, stat_in, out_v, grad_v,
+    fgp, fsum, vcol, vec, vec_in, stat, stat_in, out_v, grad_v,
     send_sems, recv_sems, local_sems,
 ):
     links = Links(send_sems, recv_sems, local_sems)
@@ -955,29 +960,21 @@
     links.greet()
     singles = (gain1_in, bias1_in, out_in, gain2_in, bias2_in, proj_in)
     first = [links.local(wq_in.at[:, mine], wq_here), links.local(tok, xt.at[r])]
+    first += [links.local(wo_in.at[mine], woa.at[r, c, mine])]
     first += [links.local(source, rows1.at[i]) for i, source in enumerate(singles)]
     first += [links.local(qv_in, qv), links.local(fc_in, fc)]
     then = [links.local(wf_in.at[mine], zf), links.local(wp_in.at[mine], zp)]
-    then += [links.local(wo_in.at[mine], woa.at[r, c, mine]), links.local(cot, gt.at[r])]
+    then += [links.local(cot, gt.at[r])]
     for copy in first:
         copy.wait()
     zq[...] = jnp.concatenate([wq_here[i] for i in range(3)], axis=1)
     pres[r] = jnp.full((8, LANES), limit[0], jnp.int32)
 
-    def column(kind, place, values):
-        spread = jnp.broadcast_to(values[None, :], (LANES, LANES))
-        colb[kind, pl.ds(place * LANES, LANES)] = spread.T
-
-    for place in range(D // LANES):
-        part = pl.ds(place * LANES, LANES)
-        for kind in range(len(singles)):
-            column(kind, place, rows1[kind, part])
-        column(Q_BIAS, place, qv[0, part])
-        column(V_BIAS, place, qv[1, part])
-        column(FC_BIAS, place, fc[pl.ds(pl.multiple_of(r * D + place * LANES, LANES), LANES)])
     links.meet()
 
     get_q = WeightGather(links, zq, mq, wqa, 3)
+    get_o = SquareGather(links, woa)
+    get_o.line(0)
     tokens = PlaneGather(links, xt, in_parts=True)
     for copy in then:
         copy.wait()
@@ -986,18 +983,33 @@
     get_f = WeightGather(links, zf, mf, wfa)
     prefixes = [links.send(pres.at[r], pres.at[r], links.plane(k)) for k in (1, 2, 3)]
     get_q.line(0)
+    get_o.line(1)
+
+    def column(kind, place, values):
+        spread = jnp.broadcast_to(values[None, :], (LANES, LANES))
+        colb[kind, pl.ds(place * LANES, LANES)] = spread.T
+
+    for place in range(D // LANES):
+        part = pl.ds(place * LANES, LANES)
+        for kind in range(len(singles)):
+            column(kind, place, rows1[kind, part])
+        column(Q_BIAS, place, qv[0, part])
+        column(V_BIAS, place, qv[1, part])
+        column(FC_BIAS, place, fc[pl.ds(pl.multiple_of(r * D + place * LANES, LANES), LANES)])
+
     tokens.relay()
-    get_o = SquareGather(links, woa)
     get_q.line(1)
+    get_o.line(2)
+    get_f.hop()
+    get_q.line(2)
+    get_o.line(3)
     get_p = WeightGather(links, zp, mp, wpa)
-    get_o.plane.relay()
-    get_q.line(2)
-    get_o.line(0)
     get_q.line(3)
     get_q.share()
+    get_f.line(0)
     tokens.finish()
-    grads = PlaneGather(links, gt)
-    get_f.hop()
+    get_o.cross()
+    grads = PlaneGather(links, gt, in_parts=True)
     get_p.hop()
     normalize(
         lambda lanes: wide(merged(xt[:, :, lanes])), fn, st1, colb.at[GAIN1], colb.at[BIAS1]
@@ -1029,42 +1041,43 @@
     def gather_head(h):
         attns.append(PlaneGather(links, at.at[:, h * HEAD_DIM : (h + 1) * HEAD_DIM]))
 
+    def get_o_relay():
+        get_o.plane.relay()
+
     attend(
         qkv,
         limit_value,
         put_attn,
         lse,
         {
-            0: [lambda: get_o.line(1)],
-            3: [lambda: get_f.line(0)],
-            4: [lambda: gather_head(0), grads.relay],
-            7: [lambda: get_o.line(2)],
+            0: [get_o_relay],
+            1: [lambda: get_f.line(1)],
+            4: [lambda: gather_head(0)],
+            7: [lambda: get_f.line(2)],
             8: [lambda: gather_head(1), lambda: attns[0].relay()],
-            10: [lambda: get_f.line(1)],
+            10: [lambda: get_p.line(0)],
         },
     )
     gather_head(2)
     attns[1].relay()
-    get_o.line(3)
-    get_o.share()
-    get_f.line(2)
-    get_p.line(0)
-    attns[2].relay()
     get_f.line(3)
     get_f.share()
+    get_o.share()
+    attns[2].relay()
+    grads.rest()
     get_p.line(1)
     get_o.finish()
     for attn in attns:
         attn.finish()
-
-    def join(i):
-        b, lanes = lax.div(i, 4), aligned(lax.rem(i, 4) * QUARTER, QUARTER)
+    grads.relay()
+
+    def join(b):
         rows = aligned(b * WIDTH, WIDTH)
-        bias = colb[OUT_BIAS, rows]
-        value = dot(merged(woa[b]), merged(at[:, :, lanes]), 0, 0)
-        mid[rows, lanes] = wide(xt[b, :, lanes]) + (value + jnp.concatenate([bias, bias], axis=1))
-
-    each(16, join)
+        bias = jnp.concatenate([colb[OUT_BIAS, rows]] * 8, axis=1)
+        value = dot(merged(woa[b]), merged(at[...]), 0, 0)
+        mid[rows, :] = wide(xt[b]) + (value + bias)
+
+    each(4, join)
     get_p.line(2)
     normalize(lambda lanes: mid[:, lanes], sn, st2, colb.at[GAIN2], colb.at[BIAS2])
     get_f.finish()
@@ -1084,9 +1097,11 @@
     grads.finish()
 
     def proj_grads(b):
-        gp[b] = low(dot(gt[b], act[...], 1, 1))
-
-    each(4, proj_grads)
+        some = aligned(b * QUARTER, QUARTER)
+        value = low(dot(merged(gt[...]), act[some, :], 1, 1))
+        gp[:, :, some] = value.reshape(4, WIDTH, QUARTER)
+
+    each(3, proj_grads)
     put_p = WeightReduce(links, gp, near_p, sum_p, up_p, dn_p, fin_p, hop_p, got_p, wp_hbm)
     get_p.finish()
 
@@ -1104,9 +1119,11 @@
             put_p.line(0)
 
     def fc_grads(b):
-        gf[b] = low(dot(sn[aligned(b * WIDTH, WIDTH), :], hg[...], 1, 1))
-
-    each(4, fc_grads)
+        some = aligned(b * QUARTER, QUARTER)
+        value = low(dot(sn[...], hg[some, :], 1, 1))
+        gf[:, :, some] = value.reshape(4, WIDTH, QUARTER)
+
+    each(3, fc_grads)
     put_f = WeightReduce(links, gf, near_f, sum_f, up_f, dn_f, fin_f, hop_f, got_f, wf_hbm)
     seconds.relay()
     put_p.line(1)
@@ -1128,6 +1145,7 @@
     vcol[...] = jnp.where(lane == V_FC + r, total, 0.0)
     put_p.line(2)
     seconds.finish()
+    outs.give(3)
 
     def back(j):
         lanes = aligned(r * QUARTER + j * LANES, LANES)
@@ -1157,11 +1175,6 @@
         links.send(ap.at[links.across(k)], dout.at[:, own], links.plane(k)) for k in (3, 1, 2)
     ]
     turns.append(links.local(ap.at[r], dout.at[:, own]))
-    swaps = [
-        links.send(br.at[links.across(k)], brf.at[:, own], links.plane(k)) for k in (3, 1, 2)
-    ]
-    swaps.append(links.local(br.at[r], brf.at[:, own]))
-
     def square_grads(b):
         value = low(dot(merged(at[:, :, own]), br[b], 1, 1))
         sq[b] = value.reshape(4, WIDTH, WIDTH)
@@ -1173,25 +1186,25 @@
     put_p.hop()
     for copy in turns:
         copy.wait()
-    for k in (3, 1, 2):
-        outs.give(k)
+    outs.give(1)
+    outs.give(2)
+    swaps = [
+        links.send(br.at[links.across(k)], brf.at[:, own], links.plane(k)) for k in (3, 1, 2)
+    ]
+    swaps.append(links.local(br.at[r], brf.at[:, own]))
     attend_back(
         qkv, limit_value, get_attn, lse, dout, dqkv, ksum, vsum,
         {
-            1: [lambda: put_o.line(0)],
+            0: [lambda: put_o.line(0)],
             2: [lambda: put_f.line(2)],
-            4: [put_p.back],
-            5: [outs.relay],
-            7: [lambda: put_o.line(1)],
+            4: [put_p.back, outs.relay],
             9: [put_f.hop, put_p.share],
-            11: [lambda: put_o.line(2)],
+            11: [lambda: put_o.line(1)],
         },
     )
-
-    def query_grads(b):
-        gq[b] = low(dot(fn[aligned(b * WIDTH, WIDTH), :], dqkv[...], 1, 1))
-
-    each(4, query_grads)
+    for some in (slice(0, 256), slice(256, 512), slice(512, WQ)):
+        value = low(dot(fn[...], dqkv[some, :], 1, 1))
+        gq[:, :, some] = value.reshape(4, WIDTH, some.stop - some.start)
     put_q = WeightReduce(links, gq, near_q, sum_q, up_q, dn_q, fin_q, hop_q, got_q, wq_hbm, 3)
 
     stat[...] = jnp.zeros_like(stat)
@@ -1200,31 +1213,35 @@
         b = links.across(k)
         rows = aligned(b * WIDTH, WIDTH)
 
+        fsum[...] = jnp.zeros_like(fsum)
+
         def first_part(j, b=b, rows=rows):
             lanes = aligned(j * QUARTER, QUARTER)
             value = dot(wqa[b], dqkv[:, lanes], 1, 0)
             fgp[b, :, lanes] = low(value)
+            gain = colb[GAIN1, rows]
             for i in range(2):
                 half = aligned(j * QUARTER + i * LANES, LANES)
                 piece = value[:, i * LANES : (i + 1) * LANES]
                 unit = wide(xt[b, :, half]) - st1[CENTER : CENTER + 1, half]
-                unit = unit * st1[INVERSE : INVERSE + 1, half]
-                weighted = piece * unit
-                gain = colb[GAIN1, rows]
+                weighted = piece * (unit * st1[INVERSE : INVERSE + 1, half])
                 stat[0:1, half] += jnp.sum(piece * gain, axis=0, keepdims=True)
                 stat[1:2, half] += jnp.sum(weighted * gain, axis=0, keepdims=True)
-                spot = lane[:WIDTH]
-                add = jnp.where(spot == V_GAIN1, jnp.sum(weighted, axis=1, keepdims=True), 0.0)
-                add = jnp.where(spot == V_BIAS1, jnp.sum(piece, axis=1, keepdims=True), add)
-                vcol[rows, :] = vcol[rows, :] + add
+                fsum[0] += weighted
+                fsum[1] += piece
 
         each(4, first_part)
         firsts.give(k)
+        spot = lane[:WIDTH]
+        add = jnp.where(spot == V_GAIN1, jnp.sum(fsum[0], axis=1, keepdims=True), 0.0)
+        add = jnp.where(spot == V_BIAS1, jnp.sum(fsum[1], axis=1, keepdims=True), add)
+        vcol[rows, :] = vcol[rows, :] + add
         if k == 3:
             put_q.add_near()
             put_q.line(0)
         elif k == 1:
             put_f.back()
+            put_o.line(2)
         elif k == 2:
             put_q.line(1)
             firsts.relay()
@@ -1322,7 +1339,7 @@
         vmem((4, 4, HALF, WIDTH), narrow), vmem((3, 4, HALF, WIDTH), narrow),
         vmem((3, 4, HALF, WIDTH), narrow), vmem((4, HALF, WIDTH), narrow),
         vmem((3, HALF, WIDTH), narrow), vmem((HALF, WIDTH), narrow),
-        vmem(sequence, narrow), vmem((D, LANES), full),
+        vmem(sequence, narrow), vmem((2, WIDTH, LANES), full), vmem((D, LANES), full),
         vmem((4, 16, D), full), vmem((7, 16, D), full), vmem((8, LEN), full), vmem((3, 8, LEN), full),
         vmem((WIDTH, LEN), narrow), vmem((WIDTH, LEN), full),
         pltpu.SemaphoreType.DMA((REMOTES,)), pltpu.SemaphoreType.DMA((REMOTES,)),

time: 154 us -> 142 us (0.922)
  Pallas kernels: 152 us -> 141 us
    pallas_call x1, Pallas kernels: 149 us -> 137 us  [run_block(): pl.pallas_call(block_kernel, out_shape=[jax.ShapeDtypeStruct(*result) for...]
where the time goes in v5:
time: 142 us
  Pallas kernels  141 us (99%)
    pallas_call x1, Pallas kernels, run_block(): pl.pallas_call(block_kernel, out_shape=[jax.ShapeDtypeStruct(*result) for...  137 us
    pallas_call x1, Pallas kernels, plane_device(): pl.pallas_call(finish_kernel, out_shape=results, in_specs=[pl.BlockSpec(m...  3.31 us

profile of v5, /device:TPU:0, one launch (start us, length us, event | category | flops | bytes accessed | tf_op | source)
XLA Modules:
  0.0 142.0 jit_solution(11492283935844381798)
XLA Ops:
  1.3 137.4 %block.1 = (bf16[192,1024]{1,0:T(8,128)(2,1)}, f32[192,1024]{1,0:T(8,128)}, bf16[192,576]{1,0:T(8,128)(2,1)}, bf16[192,768]{1,0:T(8,128)(2,1)}, bf16[192,768]{1,...) custom-call(s32[1]{0:T(128)S(6)} %copy.29.limit, bf16[192,1024]{1,0:T(8,128)(2,1)} %tok.1, f32[768]{0:T(1024)} %gain1_in.1, ...), custom_call_target="tpu_custom_call" | custom-call | tf_op jit(solution)/shard_map/block/pallas_call | solution.py:1352
  138.7 3.3 %results.1 = (bf16[192,1024]{1,0:T(8,128)(2,1)}, f32[192,1024]{1,0:T(8,128)}, f32[768]{0:T(1024)}, f32[768]{0:T(1024)}, f32[3,192,192]{2,1,0:T(8,128)}, /*index=...) custom-call(bf16[192,1024]{1,0:T(8,128)(2,1)} %get-tuple-element.21., ...), custom_call_target="tpu_custom_call" | custom-call | tf_op jit(solution)/shard_map/results/pallas_call | solution.py:1399

commit v6 on v5

--- a/solution.py
+++ b/solution.py
@@ -392,9 +392,25 @@
         for device in devices:
             pl.semaphore_signal(barrier, 1, device_id=device, device_id_type=MESH)
         self.greeted = len(devices)
+        to, since = self.routed(), self.routed_back()
+
+        @pl.when(jnp.logical_not(self.stays()))
+        def _():
+            for device in (to, since):
+                pl.semaphore_signal(barrier, 1, device_id=device, device_id_type=MESH)
 
     def meet(self):
-        pl.semaphore_wait(pltpu.get_barrier_semaphore(), self.greeted)
+        count = jnp.where(self.stays(), self.greeted, self.greeted + 2)
+        pl.semaphore_wait(pltpu.get_barrier_semaphore(), count)
+
+    def routed(self):
+        return (self.d, self.c, self.crossing(self.r, self.c))
+
+    def routed_back(self):
+        return (self.d, self.crossing(self.r, self.c), self.r)
+
+    def stays(self):
+        return jnp.logical_and(self.r == self.c, self.crossing(self.r, self.c) == self.c)
 
     def send(self, source, target, device):
         place = self.remotes
@@ -638,6 +654,25 @@
         self.shared.wait()
 
 
+class RoutedGather(WeightGather):
+    def __init__(self, links, stage, target, pieces=1):
+        self.links, self.target = links, target
+        self.mine = links.half()
+        size = HALF // pieces
+        start = links.d * HALF
+        self.rows = [pl.ds(pl.multiple_of(start + i * size, 16), size) for i in range(pieces)]
+        self.turns = [
+            Move(
+                links,
+                links.stays(),
+                stage.at[pl.ds(i * size, size)],
+                target.at[links.r, rows],
+                links.routed(),
+            )
+            for i, rows in enumerate(self.rows)
+        ]
+
+
 class SquareGather:
     def __init__(self, links, target):
         self.links, self.target = links, target
@@ -661,6 +696,10 @@
 
 
 def add_rows(target, terms):
+    if len(terms) == 2:
+        target[...] = terms[0][...] + terms[1][...]
+        return
+
     def step(i):
         place = aligned(i * 16, 16)
         total = wide(terms[0][place, :])
@@ -944,7 +983,7 @@
     limit, tok, gain1_in, bias1_in, wq_in, qv_in, wo_in, out_in, gain2_in, bias2_in,
     wf_in, fc_in, wp_in, proj_in, cot,
     out_hbm, grad_hbm, wq_hbm, wf_hbm, wp_hbm, wo_hbm, vec_hbm,
-    rows1, qv, fc, wq_here, xt, gt, wqa, wfa, wpa, woa, zq, zf, zp, mq, mf, mp, pres, colb,
+    rows1, qv, fc, wq_here, xt, gt, wqa, wfa, wpa, woa, zq, zf, zp, mf, mp, pres, colb,
     fn, qkv, at, lse, st1, st2, mid, sn, act, slope, op, hg, sp,
     x2, y2, z2, x_out, y_out, z_out, x1, y1, z1, br, ap, dout, brf, dqkv, ksum, vsum,
     gf, gp, gq, near_f, near_p, near_q, sum_f, sum_p, sum_q, up_f, up_p, up_q, dn_f, dn_p, dn_q,
@@ -972,17 +1011,16 @@
 
     links.meet()
 
-    get_q = WeightGather(links, zq, mq, wqa, 3)
+    get_q = RoutedGather(links, zq, wqa, 3)
     get_o = SquareGather(links, woa)
     get_o.line(0)
     tokens = PlaneGather(links, xt, in_parts=True)
     for copy in then:
         copy.wait()
-    get_q.hop()
+    prefixes = [links.send(pres.at[r], pres.at[r], links.plane(k)) for k in (1, 2, 3)]
+    get_q.line(0)
     tokens.rest()
     get_f = WeightGather(links, zf, mf, wfa)
-    prefixes = [links.send(pres.at[r], pres.at[r], links.plane(k)) for k in (1, 2, 3)]
-    get_q.line(0)
     get_o.line(1)
 
     def column(kind, place, values):
@@ -1114,7 +1152,7 @@
         hg[:, lanes] = low(value * slope[:, lanes])
         sp[:, lanes] = low(dot(merged(wfa[...]), hg[:, lanes], 1, 0))
         seconds.give(k)
-        if k == 3:
+        if k == 2:
             put_p.add_near()
             put_p.line(0)
 
@@ -1239,15 +1277,12 @@
         if k == 3:
             put_q.add_near()
             put_q.line(0)
-        elif k == 1:
             put_f.back()
-            put_o.line(2)
-        elif k == 2:
-            put_q.line(1)
-            firsts.relay()
     stat_sends = [links.send(stat, stat_in.at[k - 1], links.plane(k)) for k in (1, 2, 3)]
-    put_q.line(2)
-    put_o.hop()
+    put_q.line(1)
+    firsts.relay()
+    put_o.line(2)
+    put_f.share()
     rows = aligned(r * WIDTH, WIDTH)
     spot = lane[:WIDTH]
     query = jnp.zeros((WIDTH, 1), jnp.float32)
@@ -1260,11 +1295,12 @@
     vcol[rows, :] = vcol[rows, :] + add
     vec[0] = vcol[...].T[:16]
     vec_near = links.send(vec.at[0], vec_in.at[0], links.partner())
-    put_f.share()
-    put_q.hop()
+    put_q.line(2)
     vec_near.wait()
     vec[1] = vec[0] + vec_in[0]
     vec_plane = [links.send(vec.at[1], vec_in.at[k], links.plane(k)) for k in (1, 2, 3)]
+    put_o.hop()
+    put_q.hop()
     put_o.back()
     put_o.share()
     put_q.back()
@@ -1323,7 +1359,7 @@
         vmem((4, WIDTH, WQ), narrow), vmem((4, WIDTH, D), narrow), vmem((4, WIDTH, D), narrow),
         vmem((4, 4, WIDTH, WIDTH), narrow),
         vmem((HALF, WQ), narrow), vmem((HALF, D), narrow), vmem((HALF, D), narrow),
-        vmem((HALF, WQ), narrow), vmem((HALF, D), narrow), vmem((HALF, D), narrow),
+        vmem((HALF, D), narrow), vmem((HALF, D), narrow),
         vmem((4, 8, LANES), jnp.int32), vmem((9, D, LANES), full),
         vmem(tall, narrow), vmem((WQ, LEN), narrow), vmem(sequence, narrow),
         vmem((8, LEN), full), vmem((8, LEN), full), vmem((8, LEN), full),

time: 142 us -> 140 us (0.986)
  Pallas kernels: 141 us -> 138 us
    pallas_call x1, Pallas kernels: 137 us -> 135 us  [run_block(): pl.pallas_call(block_kernel, out_shape=[jax.ShapeDtypeStruct(*result) for...]
where the time goes in v6:
time: 140 us; the launch traced here: 139 us
  Pallas kernels  138 us (99%)
    pallas_call x1, Pallas kernels, run_block(): pl.pallas_call(block_kernel, out_shape=[jax.ShapeDtypeStruct(*result) for...  135 us
    pallas_call x1, Pallas kernels, plane_device(): pl.pallas_call(finish_kernel, out_shape=results, in_specs=[pl.BlockSpec(m...  3.31 us

profile of v6, /device:TPU:0, one launch (start us, length us, event | category | flops | bytes accessed | tf_op | source)
XLA Modules:
  0.0 139.5 jit_solution(13325873816229476264)
XLA Ops:
  1.3 134.9 %block.1 = (bf16[192,1024]{1,0:T(8,128)(2,1)}, f32[192,1024]{1,0:T(8,128)}, bf16[192,576]{1,0:T(8,128)(2,1)}, bf16[192,768]{1,0:T(8,128)(2,1)}, bf16[192,768]{1,...) custom-call(s32[1]{0:T(128)S(6)} %copy.29.limit, bf16[192,1024]{1,0:T(8,128)(2,1)} %tok.1, f32[768]{0:T(1024)} %gain1_in.1, ...), custom_call_target="tpu_custom_call" | custom-call | tf_op jit(solution)/shard_map/block/pallas_call | solution.py:1388
  136.2 3.3 %results.1 = (bf16[192,1024]{1,0:T(8,128)(2,1)}, f32[192,1024]{1,0:T(8,128)}, f32[768]{0:T(1024)}, f32[768]{0:T(1024)}, f32[3,192,192]{2,1,0:T(8,128)}, /*index=...) custom-call(bf16[192,1024]{1,0:T(8,128)(2,1)} %get-tuple-element.21., ...), custom_call_target="tpu_custom_call" | custom-call | tf_op jit(solution)/shard_map/results/pallas_call | solution.py:1435

commit v7 on v6

--- a/solution.py
+++ b/solution.py
@@ -1011,7 +1011,7 @@
 
     links.meet()
 
-    get_q = RoutedGather(links, zq, wqa, 3)
+    get_q = RoutedGather(links, zq, wqa, 2)
     get_o = SquareGather(links, woa)
     get_o.line(0)
     tokens = PlaneGather(links, xt, in_parts=True)

time: 140 us -> 139 us (level)
  no operation moved by 1% of the time
where the time goes in v7:
time: 139 us
  Pallas kernels  137 us (99%)
    pallas_call x1, Pallas kernels, run_block(): pl.pallas_call(block_kernel, out_shape=[jax.ShapeDtypeStruct(*result) for...  134 us
    pallas_call x1, Pallas kernels, plane_device(): pl.pallas_call(finish_kernel, out_shape=results, in_specs=[pl.BlockSpec(m...  3.31 us

profile of v7, /device:TPU:0, one launch (start us, length us, event | category | flops | bytes accessed | tf_op | source)
XLA Modules:
  0.0 138.6 jit_solution(14278243218290683707)
XLA Ops:
  1.3 133.9 %block.1 = (bf16[192,1024]{1,0:T(8,128)(2,1)}, f32[192,1024]{1,0:T(8,128)}, bf16[192,576]{1,0:T(8,128)(2,1)}, bf16[192,768]{1,0:T(8,128)(2,1)}, bf16[192,768]{1,...) custom-call(s32[1]{0:T(128)S(6)} %copy.29.limit, bf16[192,1024]{1,0:T(8,128)(2,1)} %tok.1, f32[768]{0:T(1024)} %gain1_in.1, ...), custom_call_target="tpu_custom_call" | custom-call | tf_op jit(solution)/shard_map/block/pallas_call | solution.py:1388
  135.2 3.3 %results.1 = (bf16[192,1024]{1,0:T(8,128)(2,1)}, f32[192,1024]{1,0:T(8,128)}, f32[768]{0:T(1024)}, f32[768]{0:T(1024)}, f32[3,192,192]{2,1,0:T(8,128)}, /*index=...) custom-call(bf16[192,1024]{1,0:T(8,128)(2,1)} %get-tuple-element.21., ...), custom_call_target="tpu_custom_call" | custom-call | tf_op jit(solution)/shard_map/results/pallas_call | solution.py:1435
